TPU v7x, 32 devices: a whole 2x2x4 slice. The times are simulated.
32 devices in a mesh: mem: 4 (over z), slab: 8 (over y, x, core).
Axes of the slice: x: 2, y: 2, z: 4, core: 2. Of those that a mesh axis runs over, the one named last changes fastest.
Arguments:
- ensemble: float32 [256, 256, 128], P('mem', 'slab'), may hold values from -6 to 6
- diffusivity: float32 [256, 128], P('slab'), may hold values from 0.15 to 0.25
- velocity: float32 [2, 256, 128], P(None, 'slab'), may hold values from -0.5 to 0.5
- obs_value: float32 [40960], P(('mem', 'slab')), may hold values from -6 to 6
- obs_weight: float32 [40960], P(('mem', 'slab')), may hold values from 0.3 to 12
- obs_slab: int32 [40960, 1], P(('mem', 'slab')), may hold values from 0 to 7; in each aligned block of 1280 rows (0 to 1279, 1280 to 2559, ...) at most 320 rows name the same one
- obs_cell: int32 [40960], P(('mem', 'slab')), may hold values from 0 to 1023
Outputs:
- analysis: float32 [256, 256, 128], P('mem', 'slab')
Inputs may be any that keep to these rules, and one draw needn't show every extreme that they name: `obs_slab`: among the 1280 observations stored on one device, no slab is named more than 320 times; on some device one slab is named exactly 320 times.
All inputs are finite; a program needn't handle non-finite values.
Results may differ from a plain program's by a relative error of at most 0.0085.
Values sent between devices are 32-bit elements; how exact they have to be, the bound alone decides.
No kernel may reach another device: no remote copies, remote signals or barrier semaphores. Data moves between devices by JAX's collectives and lax.ppermute only.
A program may use at most 128 MiB of HBM per device.

v0:
```python
import jax
import jax.numpy as jnp
from jax import lax
from jax.sharding import PartitionSpec as P

STEPS = 4
NS_STEPS = 5


def padded_2(shard, sides, width):
    for axis, dim in sides:
        peers, length = (lax.axis_size(axis), shard.shape[dim])
        up = [(i, (i + 1) % peers) for i in range(peers)]
        down = [(j, i) for i, j in up]
        last = lax.slice_in_dim(shard, length - width, length, axis=dim)
        leading = lax.slice_in_dim(shard, 0, width, axis=dim)
        before = lax.ppermute(last, axis, up)
        after = lax.ppermute(leading, axis, down)
        shard = jnp.concatenate([before, shard, after], axis=dim)
    return shard


def stencil(center, upper_row, lower_row, diffuse, drift_x, drift_y):
    east_side = jnp.roll(center, -1, axis=-1)
    west_side = jnp.roll(center, 1, axis=-1)
    laplace = east_side + west_side + upper_row + lower_row - 4.0 * center
    return (
        center
        + diffuse * laplace
        - 0.5 * drift_x * (east_side - west_side)
        - 0.5 * drift_y * (lower_row - upper_row)
    )


def analyse(fields, obs_vals, obs_wts, obs_cells):
    members, patches, width = fields.shape
    center_mean = jnp.mean(fields, axis=0)
    spread = (fields - center_mean[None]).astype(jnp.bfloat16)
    flat_mean = center_mean.reshape(-1)
    at_obs = jnp.take(spread.reshape(members, -1), obs_cells, axis=1)
    misfit = obs_vals - jnp.take(flat_mean, obs_cells)
    patch_of = obs_cells // width
    weights = obs_wts[None, :] * (
        patch_of[None, :] == jnp.arange(patches, dtype=jnp.int32)[:, None]
    ).astype(jnp.float32)

    def patch_gram(patch_weights):
        weighted = (at_obs * patch_weights[None, :]).astype(jnp.bfloat16)
        return jnp.einsum("mo,no->mn", weighted, at_obs, preferred_element_type=jnp.float32)

    gram = lax.map(patch_gram, weights)
    eye_f = jnp.eye(members, dtype=jnp.float32)
    system = (members - 1) * eye_f[None] + gram
    scale = 8.0 * jnp.sqrt(jnp.sum(system * system, axis=(1, 2)) / members)
    iterate = (system / scale[:, None, None]).astype(jnp.bfloat16)
    inverse_root = jnp.broadcast_to(eye_f.astype(jnp.bfloat16), iterate.shape)
    for sweep in range(NS_STEPS):
        product = jnp.einsum(
            "pij,pjk->pik", inverse_root, iterate, preferred_element_type=jnp.float32
        )
        factor = (1.5 * eye_f[None] - 0.5 * product).astype(jnp.bfloat16)
        iterate = jnp.einsum(
            "pij,pjk->pik", iterate, factor, preferred_element_type=jnp.float32
        ).astype(jnp.bfloat16)
        inverse_root = jnp.einsum(
            "pij,pjk->pik", factor, inverse_root, preferred_element_type=jnp.float32
        ).astype(jnp.bfloat16)
    root_f = inverse_root.astype(jnp.float32)
    pull = jnp.dot(
        at_obs.astype(jnp.float32), (weights * misfit[None, :]).T, precision=lax.Precision.HIGHEST
    )
    first = jnp.einsum("pij,jp->pi", root_f, pull, precision=lax.Precision.HIGHEST)
    mean_gain = (
        jnp.einsum("pij,pj->pi", root_f, first, precision=lax.Precision.HIGHEST) / scale[:, None]
    )
    transform = (
        jnp.sqrt((members - 1) / scale)[:, None, None] * root_f + mean_gain[:, None, :]
    ).astype(jnp.bfloat16)
    update = jnp.einsum("pik,kpx->ipx", transform, spread, preferred_element_type=jnp.float32)
    return center_mean[None] + update


def shards(ensemble, diffusivity, velocity, obs_value, obs_weight, obs_slab, obs_cell):
    n_slab = lax.axis_size("slab")
    local_members = ensemble.shape[0]
    rows = ensemble.shape[1]
    stacked = jnp.concatenate([ensemble, diffusivity[None], velocity], axis=0)
    padded = padded_2(stacked, (("slab", 1),), STEPS)
    fields = padded[:local_members]
    coeffs = padded[local_members:]
    length = rows + 2 * STEPS
    for step in range(STEPS):
        low_row = step + 1
        high_row = length - step - 1
        fields = stencil(
            fields[:, 1:-1],
            fields[:, :-2],
            fields[:, 2:],
            coeffs[0, low_row:high_row],
            coeffs[1, low_row:high_row],
            coeffs[2, low_row:high_row],
        )
    patch_fields = lax.all_to_all(fields, "mem", split_axis=1, concat_axis=0, tiled=True)
    obs_dev = obs_value.shape[0]
    capacity = max(2, 2 * obs_dev // n_slab)
    target = obs_slab[:, 0]
    choose = (target[:, None] == jnp.arange(n_slab, dtype=jnp.int32)[None, :]).astype(jnp.int32)
    before = jnp.cumsum(choose, axis=0) - choose
    rank_in = jnp.sum(before * choose, axis=1)
    slot = target * capacity + rank_in
    records = jnp.stack([obs_value, obs_weight, obs_cell.astype(jnp.float32)])
    outgoing = (
        jnp.zeros((3, n_slab * capacity), jnp.float32)
        .at[:, slot]
        .set(records)
        .reshape(3, n_slab, capacity)
    )
    buffer = lax.all_to_all(outgoing, "slab", split_axis=1, concat_axis=1, tiled=True).reshape(
        3, n_slab * capacity
    )
    analysed = analyse(patch_fields, buffer[0], buffer[1], buffer[2].astype(jnp.int32))
    return lax.all_to_all(analysed, "mem", split_axis=0, concat_axis=1, tiled=True)


def solution(mesh):
    return jax.shard_map(
        shards,
        mesh=mesh,
        in_specs=(
            P("mem", "slab", None),
            P("slab", None),
            P(None, "slab", None),
            P(("mem", "slab")),
            P(("mem", "slab")),
            P(("mem", "slab"), None),
            P(("mem", "slab")),
        ),
        out_specs=P("mem", "slab", None),
        check_vma=False,
    )
```

profile of v0, /device:TPU:0, one launch (start us, length us, event | category | flops | bytes accessed | tf_op | source)
XLA Modules:
  0.0 167.0 jit_solution(17399415933805119149)
XLA Ops:
  0.0 1.8 %copy.26 = f32[64,32,128]{2,0,1:T(8,128)S(1)} copy(f32[64,32,128]{2,1,0:T(8,128)} %param.9) | data formatting | bytes 2097152 | tf_op args[0]
  2.0 0.7 pad_maximum_fusion.11
  2.7 0.5 collective-permute-start
  3.2 2.9 %collective-permute-start.1 = (f32[67,4,128]{2,0,1:T(8,128)}, f32[67,4,128]{2,0,1:T(8,128)S(1)}, u32[]{:S(2)}, u32[]{:S(2)}) collective-permute-start(f32[67,4,128]{2,0,1:T(8,128)} %get-tuple-element.82), channel_id=1, source_target_pairs={{1,0},{2,1},{3,2},{4,3},{5,4},{6,5},{7,6},{0,7},{9,8},{10,9},{11,1... | collective-permute-start | bytes 411656 | tf_op jit(solution)/shard_map/ppermute | solution.py:18
  6.1 2.3 %reduce-window.6 = s32[8,10,128]{2,1,0:T(8,128)S(1)} reduce-window(s32[8,10,128]{2,1,0:T(8,128)S(1)} %fusion.18, s32[]{:T(128)} %copy.89), window={size=1x1x128 pad=0_0x0_0x127_0}, to_apply=%region_1.2 | reduce-window | flops 1300480 | bytes 81924 | tf_op jit(solution)/shard_map/reduce-window
  9.4 6.4 %scatter_custom_fusion = f32[3,2560]{0,1:T(8,128)S(1)} fusion(s32[1280]{0:T(1024)S(1)} %fusion.32, f32[1280,3]{1,0:T(8,128)S(1)} %copy.30, f32[]{:T(128)} %constant.42.clone.1), kind=kCustom, calls=%fused_computation.50 | custom fusion | bytes 30724 | tf_op jit(solution)/shard_map/scatter | solution.py:115
  15.8 1.1 copy.31
  16.9 3.6 %all-to-all-start.1 = ((f32[3,8,320]{2,0,1:T(4,128)}), f32[3,8,320]{2,0,1:T(4,128)S(1)}, u32[]{:S(2)}, u32[]{:S(2)}) async-start(f32[3,8,320]{2,0,1:T(4,128)} %copy.31), calls=%async_computation.1 | async-start | bytes 98304 | tf_op jit(solution)/shard_map/all_to_all | solution.py:118
  20.5 0.6 multiply_bitcast_fusion.1
  21.1 0.7 fusion.15
  22.9 1.2 multiply_subtract_fusion
  25.1 1.2 multiply_subtract_fusion.1
  27.2 1.1 multiply_subtract_fusion.2
  29.4 1.9 %multiply_subtract_fusion.3 = f32[64,32,128]{2,0,1:T(8,128)} fusion(f32[64,34,128]{2,0,1:T(8,128)S(1)} %multiply_subtract_fusion.2, f32[64,32,127]{2,0,1:T(8,128)S(1)} %get-tuple-element.78, f32[64,32,1]{2,0,1:T(8,128)S(1)} %get-tuple-element.80, f32[64,32,1]{2,0,1:T(8,128)S(1)} %get-tuple-element.79, f32[64,32,127]{2,0,1:T(8,128)S(1)} %get-tuple-element.77, ...), kind=kLoop, calls=%fused_computation.49 | loop fusion | flops 3932160 | bytes 6340608 | tf_op jit(solution)/shard_map/sub | solution.py:28
  31.3 0.6 copy-done.6
  32.0 5.4 %all-to-all-start = ((f32[64,32,128]{2,0,1:T(8,128)}), f32[64,32,128]{2,0,1:T(8,128)S(1)}, u32[]{:S(2)}, u32[]{:S(2)}) async-start(f32[64,32,128]{2,0,1:T(8,128)} %multiply_subtract_fusion.3), calls=%async_computation | async-start | bytes 2097152 | tf_op jit(solution)/shard_map/all_to_all | solution.py:103
  37.4 0.7 fusion.14
  38.1 0.8 fusion.25
  39.1 0.9 slice_reduce_fusion.1
  40.3 0.6 fusion.17
  40.9 22.8 %all-to-all-done = f32[64,32,128]{2,0,1:T(8,128)S(1)} async-done(((f32[64,32,128]{2,0,1:T(8,128)}), f32[64,32,128]{2,0,1:T(8,128)S(1)}, u32[]{:S(2)}, u32[]{:S(2)}) %all-to-all-start) | async-done | bytes 1048608 | tf_op jit(solution)/shard_map/all_to_all | solution.py:103
  63.7 1.6 copy.29
  65.2 1.8 %copy.44 = f32[4,64,8,128]{1,0,3,2:T(4,128)} copy(f32[4,64,8,128]{3,1,2,0:T(8,128)S(1)} %bitcast.118) | data formatting | bytes 2097152 | tf_op jit(solution)/shard_map/all_to_all | solution.py:103
  67.1 0.5 bitcast_reduce_fusion
  67.6 3.2 %reshape.163 = f32[256,1024]{0,1:T(8,128)} reshape(f32[4,64,8,128]{1,0,3,2:T(4,128)} %copy.44) | data formatting | bytes 2097152 | tf_op jit(solution)/shard_map/all_to_all | solution.py:103
  70.8 9.4 %gather_fusion.1 = f32[2560]{0:T(1024)S(1)} fusion(f32[1024]{0:T(1024)S(1)} %get-tuple-element.86, s32[3072]{0:T(1024)S(1)} %pad_clamp_fusion), kind=kCustom, calls=%fused_computation.1 | custom fusion | bytes 30720 | tf_op jit(solution)/shard_map/jit(_take)/gather | solution.py:41
  80.2 1.4 subtract_convert_fusion.5
  81.7 8.1 %gather_fusion = bf16[2560,256]{1,0:T(8,128)(2,1)} fusion(bf16[256,1024]{0,1:T(8,128)(2,1)S(1)} %subtract_convert_fusion.5, s32[3072]{0:T(1024)S(1)} %pad_clamp_fusion), kind=kCustom, calls=%fused_computation | custom fusion | bytes 2631680 | tf_op jit(solution)/shard_map/jit(_take)/gather | solution.py:40
  89.8 0.6 select_subtract_fusion
  90.4 0.6 copy-done.13
  91.0 2.4 %fusion.10 = bf16[256,2560]{0,1:T(8,128)(2,1)S(1)} fusion(bf16[2560,256]{1,0:T(8,128)(2,1)} %gather_fusion, pred[2560]{0:T(1024)(128)(4,1)S(1)} %get-tuple-element.55), kind=kLoop, calls=%fused_computation.52 | loop fusion | flops 655360 | bytes 2624000 | tf_op jit(solution)/shard_map/jit(_take)/select_n | solution.py:40
  93.4 1.6 copy.34
  95.0 25.8 %while.10 = (s32[]{:T(128)}, f32[8,256,256]{2,1,0:T(8,128)S(1)}, bf16[256,2560]{1,0:T(8,128)(2,1)}, f32[8,2560]{1,0:T(8,128)}, s32[]{:T(128)}) while((s32[]{:T(128)}, f32[8,256,256]{2,1,0:T(8,128)S(1)}, bf16[256,2560]{1,0:T(8,128)(2,1)}, f32[8,2560]{1,0:T(8,128)}, s32[]{:T(128)}) %tuple.45), condition=%wide.region_6.7_spmd, body=%wide.region_5.6_spmd.sunk | while | flops 337510400 | bytes 2916929 | solution.py:51
  95.0 1.0 dynamic-slice_reduce_fusion.2
  96.0 2.3 %fusion.75 = f32[8,256,256]{2,1,0:T(8,128)S(1)} fusion(f32[8,256,256]{2,1,0:T(8,128)S(1)} %get-tuple-element.126, s32[]{:T(128)} %get-tuple-element.125, bf16[256,2560]{1,0:T(8,128)(2,1)} %get-tuple-element.132, f32[2560]{0:T(1024)S(1)} %dynamic-slice_reduce_fusion.2), kind=kOutput, calls=%fused_computation.7.clone.1 | convolution fusion | flops 337510400 | bytes 2896384 | tf_op jit(solution)/shard_map/while/body/eval_jaxpr/mo,no->mn/dot_general | solution.py:49
  98.3 0.9 dynamic-slice_reduce_fusion.2
  99.2 2.3 %fusion.75 = f32[8,256,256]{2,1,0:T(8,128)S(1)} fusion(f32[8,256,256]{2,1,0:T(8,128)S(1)} %get-tuple-element.126, s32[]{:T(128)} %get-tuple-element.125, bf16[256,2560]{1,0:T(8,128)(2,1)} %get-tuple-element.132, f32[2560]{0:T(1024)S(1)} %dynamic-slice_reduce_fusion.2), kind=kOutput, calls=%fused_computation.7.clone.1 | convolution fusion | flops 337510400 | bytes 2896384 | tf_op jit(solution)/shard_map/while/body/eval_jaxpr/mo,no->mn/dot_general | solution.py:49
  101.5 0.9 dynamic-slice_reduce_fusion.2
  102.4 2.3 %fusion.75 = f32[8,256,256]{2,1,0:T(8,128)S(1)} fusion(f32[8,256,256]{2,1,0:T(8,128)S(1)} %get-tuple-element.126, s32[]{:T(128)} %get-tuple-element.125, bf16[256,2560]{1,0:T(8,128)(2,1)} %get-tuple-element.132, f32[2560]{0:T(1024)S(1)} %dynamic-slice_reduce_fusion.2), kind=kOutput, calls=%fused_computation.7.clone.1 | convolution fusion | flops 337510400 | bytes 2896384 | tf_op jit(solution)/shard_map/while/body/eval_jaxpr/mo,no->mn/dot_general | solution.py:49
  104.7 0.9 dynamic-slice_reduce_fusion.2
  105.7 2.3 %fusion.75 = f32[8,256,256]{2,1,0:T(8,128)S(1)} fusion(f32[8,256,256]{2,1,0:T(8,128)S(1)} %get-tuple-element.126, s32[]{:T(128)} %get-tuple-element.125, bf16[256,2560]{1,0:T(8,128)(2,1)} %get-tuple-element.132, f32[2560]{0:T(1024)S(1)} %dynamic-slice_reduce_fusion.2), kind=kOutput, calls=%fused_computation.7.clone.1 | convolution fusion | flops 337510400 | bytes 2896384 | tf_op jit(solution)/shard_map/while/body/eval_jaxpr/mo,no->mn/dot_general | solution.py:49
  107.9 0.9 dynamic-slice_reduce_fusion.2
  108.9 2.3 %fusion.75 = f32[8,256,256]{2,1,0:T(8,128)S(1)} fusion(f32[8,256,256]{2,1,0:T(8,128)S(1)} %get-tuple-element.126, s32[]{:T(128)} %get-tuple-element.125, bf16[256,2560]{1,0:T(8,128)(2,1)} %get-tuple-element.132, f32[2560]{0:T(1024)S(1)} %dynamic-slice_reduce_fusion.2), kind=kOutput, calls=%fused_computation.7.clone.1 | convolution fusion | flops 337510400 | bytes 2896384 | tf_op jit(solution)/shard_map/while/body/eval_jaxpr/mo,no->mn/dot_general | solution.py:49
  111.2 0.9 dynamic-slice_reduce_fusion.2
  112.1 2.3 %fusion.75 = f32[8,256,256]{2,1,0:T(8,128)S(1)} fusion(f32[8,256,256]{2,1,0:T(8,128)S(1)} %get-tuple-element.126, s32[]{:T(128)} %get-tuple-element.125, bf16[256,2560]{1,0:T(8,128)(2,1)} %get-tuple-element.132, f32[2560]{0:T(1024)S(1)} %dynamic-slice_reduce_fusion.2), kind=kOutput, calls=%fused_computation.7.clone.1 | convolution fusion | flops 337510400 | bytes 2896384 | tf_op jit(solution)/shard_map/while/body/eval_jaxpr/mo,no->mn/dot_general | solution.py:49
  114.4 0.9 dynamic-slice_reduce_fusion.2
  115.3 2.3 %fusion.75 = f32[8,256,256]{2,1,0:T(8,128)S(1)} fusion(f32[8,256,256]{2,1,0:T(8,128)S(1)} %get-tuple-element.126, s32[]{:T(128)} %get-tuple-element.125, bf16[256,2560]{1,0:T(8,128)(2,1)} %get-tuple-element.132, f32[2560]{0:T(1024)S(1)} %dynamic-slice_reduce_fusion.2), kind=kOutput, calls=%fused_computation.7.clone.1 | convolution fusion | flops 337510400 | bytes 2896384 | tf_op jit(solution)/shard_map/while/body/eval_jaxpr/mo,no->mn/dot_general | solution.py:49
  117.6 0.9 dynamic-slice_reduce_fusion.2
  118.6 2.3 %fusion.75 = f32[8,256,256]{2,1,0:T(8,128)S(1)} fusion(f32[8,256,256]{2,1,0:T(8,128)S(1)} %get-tuple-element.126, s32[]{:T(128)} %get-tuple-element.125, bf16[256,2560]{1,0:T(8,128)(2,1)} %get-tuple-element.132, f32[2560]{0:T(1024)S(1)} %dynamic-slice_reduce_fusion.2), kind=kOutput, calls=%fused_computation.7.clone.1 | convolution fusion | flops 337510400 | bytes 2896384 | tf_op jit(solution)/shard_map/while/body/eval_jaxpr/mo,no->mn/dot_general | solution.py:49
  121.2 0.6 divide_sqrt_fusion
  121.8 0.6 divide_convert_fusion
  124.1 0.5 subtract_convert_fusion.3
  125.4 0.5 subtract_convert_fusion.2
  126.8 0.8 copy-done
  127.7 0.9 convolution_bitcast_fusion
  128.5 0.5 subtract_convert_fusion.1
  129.0 1.0 copy-done.3
  130.4 2.9 %subtract_convert_fusion = bf16[8,256,256]{2,1,0:T(8,128)(2,1)} fusion(bf16[8,256,256]{2,1,0:T(8,128)(2,1)S(1)} %convolution_convert_fusion.2, bf16[8,256,256]{2,1,0:T(8,128)(2,1)S(1)} %convolution_convert_fusion.3, bf16[8,256,256]{2,1,0:T(8,128)(2,1)} %copy-done.3, f32[256,256]{1,0:T(8,128)S(1)} %copy-done.5), kind=kOutput, calls=%fused_computation.10 | convolution fusion | flops 538968064 | bytes 4456448 | tf_op jit(solution)/shard_map/pij,pjk->pik/dot_general | solution.py:58
  133.4 1.7 convolution_convert_fusion
  135.0 0.9 fusion.30
  136.0 0.9 fusion.28
  137.1 0.6 fusion.4
  138.1 27.9 %all_to_all.44 = f32[256,8,128]{2,1,0:T(8,128)S(1)} all-to-all(f32[256,8,128]{2,1,0:T(8,128)S(1)} %copy.36), channel_id=1, replica_groups=mesh['mem'=4,'slab'=8] {'mem'}, dimensions={0} | all-to-all | bytes 2097152 | tf_op jit(solution)/shard_map/all_to_all | solution.py:122
  165.9 1.1 copy.76
  (96 shorter events, 10.1 us)
Async XLA Ops:
  0.0 1.9 %copy-start.7 = (f32[2,32,128]{2,1,0:T(8,128)S(1)}, f32[2,32,128]{2,1,0:T(8,128)}, u32[]{:S(2)}) copy-start(f32[2,32,128]{2,1,0:T(8,128)} %param.11) | copy-start | bytes 98308
  0.0 1.9 %copy-start.4 = (f32[32,128]{1,0:T(8,128)S(1)}, f32[32,128]{1,0:T(8,128)}, u32[]{:S(2)}) copy-start(f32[32,128]{1,0:T(8,128)} %param.10) | copy-start | bytes 49156
  1.9 4.2 %copy-start.11 = (s32[1280,1]{0,1:T(1,128)S(1)}, s32[1280,1]{0,1:T(1,128)}, u32[]{:S(2)}) copy-start(s32[1280,1]{0,1:T(1,128)} %param.14) | copy-start | bytes 15364
  1.9 7.1 %copy-start.15 = (s32[1280]{0:T(1024)S(1)}, s32[1280]{0:T(1024)}, u32[]{:S(2)}) copy-start(s32[1280]{0:T(1024)} %param.15) | copy-start | bytes 15364
  1.9 7.1 %copy-start.16 = (f32[1280]{0:T(1024)S(1)}, f32[1280]{0:T(1024)}, u32[]{:S(2)}) copy-start(f32[1280]{0:T(1024)} %param.12) | copy-start | bytes 15364
  1.9 7.2 %copy-start.17 = (f32[1280]{0:T(1024)S(1)}, f32[1280]{0:T(1024)}, u32[]{:S(2)}) copy-start(f32[1280]{0:T(1024)} %param.13) | copy-start | bytes 15364
  2.7 19.1 %collective-permute-start = (f32[67,4,128]{2,0,1:T(8,128)}, f32[67,4,128]{2,0,1:T(8,128)S(1)}, u32[]{:S(2)}, u32[]{:S(2)}) collective-permute-start(f32[67,4,128]{2,0,1:T(8,128)} %get-tuple-element.81), channel_id=1, source_target_pairs={{0,1},{1,2},{2,3},{3,4},{4,5},{5,6},{6,7},{7,0},{8,9},{9,10},{10,1... | collective-permute-start | bytes 411656 | tf_op jit(solution)/shard_map/ppermute | solution.py:17
  3.2 18.6 %collective-permute-start.1 = (f32[67,4,128]{2,0,1:T(8,128)}, f32[67,4,128]{2,0,1:T(8,128)S(1)}, u32[]{:S(2)}, u32[]{:S(2)}) collective-permute-start(f32[67,4,128]{2,0,1:T(8,128)} %get-tuple-element.82), channel_id=1, source_target_pairs={{1,0},{2,1},{3,2},{4,3},{5,4},{6,5},{7,6},{0,7},{9,8},{10,9},{11,1... | collective-permute-start | bytes 411656 | tf_op jit(solution)/shard_map/ppermute | solution.py:18
  16.9 14.4 %all-to-all-start.1 = ((f32[3,8,320]{2,0,1:T(4,128)}), f32[3,8,320]{2,0,1:T(4,128)S(1)}, u32[]{:S(2)}, u32[]{:S(2)}) async-start(f32[3,8,320]{2,0,1:T(4,128)} %copy.31), calls=%async_computation.1 | async-start | bytes 98304 | tf_op jit(solution)/shard_map/all_to_all | solution.py:118
  28.7 0.7 copy-start.8
  31.3 0.6 copy-start.6
  32.0 31.7 %all-to-all-start = ((f32[64,32,128]{2,0,1:T(8,128)}), f32[64,32,128]{2,0,1:T(8,128)S(1)}, u32[]{:S(2)}, u32[]{:S(2)}) async-start(f32[64,32,128]{2,0,1:T(8,128)} %multiply_subtract_fusion.3), calls=%async_computation | async-start | bytes 2097152 | tf_op jit(solution)/shard_map/all_to_all | solution.py:103
  40.3 26.8 %copy-start.9 = (s32[2560]{0:T(1024)}, s32[2560]{0:T(1024)S(1)}, u32[]{:S(2)}) copy-start(s32[2560]{0:T(1024)S(1)} %add_select_fusion) | copy-start | bytes 30724
  90.4 0.6 copy-start.13
  95.0 25.8 %copy-start.2 = (f32[256,256]{1,0:T(8,128)S(1)}, f32[256,256]{1,0:T(8,128)}, u32[]{:S(2)}) copy-start(f32[256,256]{1,0:T(8,128)} %fusion.15) | copy-start | bytes 786436
  121.8 0.6 copy-start.18
  121.8 1.0 copy-start.5
  126.4 1.3 copy-start
  126.4 1.3 copy-start.10
  126.4 1.3 copy-start.12
  126.4 1.3 copy-start.14
  129.0 1.0 copy-start.3
  135.0 1.9 %copy-start.19 = (f32[8]{0:T(128)S(1)}, f32[8]{0:T(128)}, u32[]{:S(2)}) copy-start(f32[8]{0:T(128)} %copy-done.18) | copy-start | bytes 100
  135.0 1.9 %copy-start.1 = (f32[4,64,8,128]{3,2,1,0:T(8,128)S(1)}, f32[4,64,8,128]{3,2,1,0:T(8,128)}, u32[]{:S(2)}) copy-start(f32[4,64,8,128]{3,2,1,0:T(8,128)} %copy.29) | copy-start | bytes 3145732
  136.0 1.1 copy-start.20
where the time goes:
time: 168 us; the launch traced here: 167 us
  local copies, waits for them, and re-layouts  52.9 us (31%)
  matrix products  31 us (18%)
  blocking collectives  27.9 us (17%)
  waiting for transfers between devices  22.8 us (14%)
  other arithmetic  19.4 us (12%)
  starting transfers between devices  12.3 us (7%)
    all_to_all x1, blocking collectives, shards(): lax.all_to_all(analysed, 'mem', split_axis=0, concat_axis=1, tiled=True)  27.9 us
    all_to_all x1, waiting for transfers between devices, shards(): lax.all_to_all(fields, 'mem', split_axis=1, concat_axis=0, tiled=True)  22.8 us
    dot_general x8, matrix products, patch_gram(): jnp.einsum('mo,no->mn', weighted, at_obs, preferred_element_type=jnp.floa...  18.2 us
    gather x1, local copies, waits for them, and re-layouts, analyse(): misfit = obs_vals - jnp.take(flat_mean, obs_cells)  9.38 us
    gather x1, local copies, waits for them, and re-layouts, analyse(): at_obs = jnp.take(spread.reshape(members, -1), obs_cells, axis=1)  8.14 us
    dynamic_slice x8, local copies, waits for them, and re-layouts, analyse(): gram = lax.map(patch_gram, weights)  7.44 us
    all_to_all x3, local copies, waits for them, and re-layouts, shards(): lax.all_to_all(fields, 'mem', split_axis=1, concat_axis=0, tiled=True)  6.61 us
    scatter x1, local copies, waits for them, and re-layouts, shards(): outgoing = jnp.zeros((3, n_slab * capacity), jnp.float32).at[:, slot].set...  6.44 us
  transfers between devices with their start and end apart: 4, of which 1 were waited for; matrix products, arithmetic and copies ran while one was open for 15% of the time, Pallas kernels for 0%

commit v1 on v0

v1 whole, which is shorter than its diff:
```python
import functools

import jax
import jax.numpy as jnp
from jax import lax
from jax.experimental import pallas as pl
from jax.experimental.pallas import tpu as pltpu
from jax.sharding import PartitionSpec as P

STEPS = 4
NS_STEPS = 5
HALF = 4
SUB = 8
F32 = jnp.float32
BF16 = jnp.bfloat16

VMEM = pl.BlockSpec(memory_space=pltpu.VMEM)
SMEM = pl.BlockSpec(memory_space=pltpu.SMEM)


def edge_kernel(top_ref, bottom_ref, coef_ref, head_ref, tail_ref):
    members = top_ref.shape[0]
    rows = coef_ref.shape[1]
    for r in range(STEPS):
        head_ref[r, :members, :] = top_ref[:, 0, r, :]
        tail_ref[r, :members, :] = bottom_ref[:, 0, SUB - STEPS + r, :]
        for k in range(3):
            head_ref[r, members + k : members + k + 1, :] = coef_ref[k, r : r + 1, :]
            tail_ref[r, members + k : members + k + 1, :] = coef_ref[
                k, rows - STEPS + r : rows - STEPS + r + 1, :
            ]


def edges(ens, coefs):
    members, groups = ens.shape[:2]
    width = ens.shape[-1]
    shape = jax.ShapeDtypeStruct((STEPS, members + SUB, width), F32)
    block = (members, 1, SUB, width)
    return pl.pallas_call(
        edge_kernel,
        grid=(1,),
        in_specs=[
            pl.BlockSpec(block, lambda i: (0, 0, 0, 0)),
            pl.BlockSpec(block, lambda i: (0, groups - 1, 0, 0)),
            pl.BlockSpec(coefs.shape, lambda i: (0, 0, 0)),
        ],
        out_specs=[pl.BlockSpec(shape.shape, lambda i: (0, 0, 0))] * 2,
        out_shape=[shape] * 2,
        name="edges",
    )(ens, ens, coefs)


def forecast_kernel(chunk, n_mem, *refs):
    if chunk:
        place, ens_ref, coef_ref, above_ref, below_ref = refs[:5]
        refs = refs[5:]
    else:
        place, ens_ref, coef_ref = refs[:3]
        refs = refs[3:]
    outs, field, table = refs[:n_mem], refs[n_mem], refs[n_mem + 1]
    members, groups, _, width = ens_ref.shape
    rows = groups * SUB

    for g in range(groups):
        for r in range(SUB):
            field[STEPS + g * SUB + r] = ens_ref[:, g, r, :]

    def put_table(first, diffuse, drift_x, drift_y):
        count = diffuse.shape[0]
        parts = (
            1.0 - 4.0 * diffuse,
            diffuse - 0.5 * drift_x,
            diffuse + 0.5 * drift_x,
            diffuse + 0.5 * drift_y,
            diffuse - 0.5 * drift_y,
        )
        for r in range(count):
            for k, part in enumerate(parts):
                table[first + r, k] = jnp.broadcast_to(part[r : r + 1], (SUB, width))

    put_table(STEPS, coef_ref[0], coef_ref[1], coef_ref[2])
    if chunk:
        for first, edge in ((0, above_ref), (STEPS + rows, below_ref)):
            for r in range(STEPS):
                field[first + r] = edge[r, :members, :]
                put_table(
                    first + r,
                    edge[r, members : members + 1, :],
                    edge[r, members + 1 : members + 2, :],
                    edge[r, members + 2 : members + 3, :],
                )

    for shift in range(n_mem):
        group = lax.rem(place[0] + shift, n_mem)
        if chunk:
            start = jnp.where(group == 0, 0, group * SUB + STEPS)
        else:
            start = jnp.where(group == 0, STEPS, group * SUB)

        def some_members(b, carry, start=start, out=outs[shift]):
            at = pl.ds(pl.multiple_of(b * SUB, SUB), SUB)
            now = [field[start + i, at, :] for i in range(HALF + 2 * STEPS)]
            for step in range(STEPS):
                after = []
                for i in range(1, len(now) - 1):
                    row = start + step + i
                    center = now[i]
                    east = pltpu.roll(center, width - 1, 1)
                    west = pltpu.roll(center, 1, 1)
                    after.append(
                        (center * table[row, 0] + east * table[row, 1])
                        + (west * table[row, 2] + now[i - 1] * table[row, 3])
                        + now[i + 1] * table[row, 4]
                    )
                now = after
            for i in range(HALF):
                out[i, at, :] = now[i]
            return carry

        lax.fori_loop(0, members // SUB, some_members, 0)


def forecast(chunk, n_mem, place, ens, coefs, halos=()):
    members, groups, _, width = ens.shape
    rows = groups * SUB
    shape = jax.ShapeDtypeStruct((HALF, members, width), F32)
    return pl.pallas_call(
        functools.partial(forecast_kernel, chunk, n_mem),
        in_specs=[SMEM] + [VMEM] * (2 + len(halos)),
        out_specs=[VMEM] * n_mem,
        out_shape=[shape] * n_mem,
        scratch_shapes=[
            pltpu.VMEM((rows + 2 * STEPS, members, width), F32),
            pltpu.VMEM((rows + 2 * STEPS, 5, SUB, width), F32),
        ],
        name=f"forecast{chunk}",
    )(place, ens, coefs, *halos)


def tally_kernel(value_ref, weight_ref, slab_ref, cell_ref, out_ref):
    blocks, lanes = value_ref.shape
    bins = out_ref.shape[1]
    width = out_ref.shape[2]
    bin_id = lax.broadcasted_iota(jnp.int32, (bins, lanes), 0)
    column_id = lax.broadcasted_iota(jnp.int32, (width, lanes), 0)
    totals = jnp.zeros((2 * bins, width), F32)
    for b in range(blocks):
        cell = cell_ref[b : b + 1, :]
        weight = weight_ref[b : b + 1, :]
        product = weight * value_ref[b : b + 1, :]
        named = slab_ref[b : b + 1, :] * SUB + cell // width
        here = bin_id == named
        column = jnp.where(column_id == cell % width, 1.0, 0.0).astype(BF16)
        rest = jnp.concatenate(
            [jnp.where(here, weight, 0.0), jnp.where(here, product, 0.0)], axis=0
        )
        for _ in range(3):
            piece = rest.astype(BF16)
            rest = rest - piece.astype(F32)
            totals = totals + lax.dot_general(
                piece, column, (((1,), (1,)), ((), ())), preferred_element_type=F32
            )
    out_ref[0] = totals[:bins]
    out_ref[1] = totals[bins:]


def tally(value, weight, slab, cell, n_slab, width):
    lanes = 128
    return pl.pallas_call(
        tally_kernel,
        in_specs=[VMEM] * 4,
        out_specs=VMEM,
        out_shape=jax.ShapeDtypeStruct((2, n_slab * SUB, width), F32),
        name="tally",
    )(*(a.reshape(-1, lanes) for a in (value, weight, slab, cell)))


def halves(a):
    high = a.astype(BF16)
    return high, (a - high.astype(F32)).astype(BF16)


def left(a):
    return jnp.concatenate(halves(a), axis=1)


def right(b):
    both = jnp.concatenate(halves(b), axis=1)
    return jnp.concatenate([both, both], axis=0)


def product(a, b):
    both = jnp.dot(a, b, preferred_element_type=F32)
    width = both.shape[1] // 2
    return both[:, :width] + both[:, width:]


def analyse_kernel(chunk, n_mem, place, tallies_ref, *refs):
    fields, outs, spread = refs[:n_mem], refs[n_mem : 2 * n_mem], refs[2 * n_mem]
    local, width = fields[0].shape[1:]
    members = n_mem * local
    n_slab = tallies_ref.shape[0]
    eye = lax.broadcasted_iota(jnp.int32, (width, width), 0) == lax.broadcasted_iota(
        jnp.int32, (width, width), 1
    )
    total = tallies_ref[0]
    for k in range(1, n_slab):
        total = total + tallies_ref[k]
    first_half = (place[0] == 0) if chunk else (place[0] != 0)
    total = jnp.where(first_half, total[:, :HALF], total[:, HALF:])
    patches = range(HALF)

    means, grams, iterates, scales, gaps = [], [], [], [], []
    for p in patches:
        weight = total[0, p : p + 1, :]
        mean = sum(jnp.sum(f[p], axis=0, keepdims=True) for f in fields) * (1.0 / members)
        for k, f in enumerate(fields):
            spread[p, k * local : (k + 1) * local, :] = (f[p] - mean).astype(BF16)
        s = spread[p]
        gram = lax.dot_general(s, s, (((0,), (0,)), ((), ())), preferred_element_type=F32)
        scaled = gram * weight
        trace = jnp.sum(jnp.where(eye, scaled, 0.0), keepdims=True)
        square = jnp.sum(scaled * scaled.T, keepdims=True)
        norm = (members - 1.0) ** 2 * members + 2.0 * (members - 1.0) * trace + square
        scale = 8.0 * jnp.sqrt(norm * (1.0 / members))
        inverse = 1.0 / scale
        iterates.append(scaled * inverse + jnp.where(eye, (members - 1.0) * inverse, 0.0))
        means.append(mean)
        grams.append(gram)
        scales.append(inverse)
        gaps.append(total[1, p : p + 1, :] - weight * mean)

    roots = [None] * HALF
    for step in range(NS_STEPS):
        last = step == NS_STEPS - 1
        if step == 0:
            both = iterates
        else:
            rights = [right(y) for y in iterates]
            both = [product(left(roots[p]), rights[p]) for p in patches]
        factors = [jnp.where(eye, 1.5, 0.0) - 0.5 * b for b in both]
        lefts = [left(f) for f in factors]
        if not last:
            iterates = [
                product(lefts[p], right(iterates[p]) if step == 0 else rights[p]) for p in patches
            ]
        if step == 0:
            roots = factors
        else:
            roots = [product(lefts[p], right(roots[p])) for p in patches]

    for p in patches:
        root = right(roots[p])
        line = jnp.broadcast_to(gaps[p], (SUB, width))
        line = product(left(line), root)
        line = product(left(line), root)
        line = product(left(line), right(grams[p]))
        base = means[p] + line[:1] * scales[p]
        transform = (jnp.sqrt((members - 1.0) * scales[p]) * roots[p]).astype(BF16)
        update = lax.dot_general(
            spread[p], transform, (((1,), (1,)), ((), ())), preferred_element_type=F32
        )
        for k, out in enumerate(outs):
            out[p] = base + update[k * local : (k + 1) * local]


def analyse(chunk, n_mem, place, tallies, fields):
    shape = jax.ShapeDtypeStruct(fields[0].shape, F32)
    local, width = fields[0].shape[1:]
    return pl.pallas_call(
        functools.partial(analyse_kernel, chunk, n_mem),
        in_specs=[SMEM] + [VMEM] * (1 + n_mem),
        out_specs=[VMEM] * n_mem,
        out_shape=[shape] * n_mem,
        scratch_shapes=[pltpu.VMEM((HALF, n_mem * local, width), BF16)],
        name=f"analyse{chunk}",
    )(place, tallies, *fields)


def gather_kernel(n_mem, place, *refs):
    early, late, out_ref = refs[:n_mem], refs[n_mem : 2 * n_mem], refs[2 * n_mem]
    for shift in range(n_mem):
        group = lax.rem(place[0] + shift, n_mem)
        for r in range(HALF):
            a, b = early[shift][r], late[shift][r]
            out_ref[:, group, r, :] = jnp.where(group == 0, b, a)
            out_ref[:, group, HALF + r, :] = jnp.where(group == 0, a, b)


def gather(n_mem, place, early, late):
    local, width = early[0].shape[1:]
    block = min(local, 2 * SUB)
    part = pl.BlockSpec((HALF, block, width), lambda i: (0, i, 0))
    return pl.pallas_call(
        functools.partial(gather_kernel, n_mem),
        grid=(local // block,),
        in_specs=[SMEM] + [part] * (2 * n_mem),
        out_specs=pl.BlockSpec((block, n_mem, SUB, width), lambda i: (i, 0, 0, 0)),
        out_shape=jax.ShapeDtypeStruct((local, n_mem, SUB, width), F32),
        name="gather",
    )(place, *early, *late)


def shards(ensemble, diffusivity, velocity, obs_value, obs_weight, obs_slab, obs_cell):
    n_slab, n_mem = lax.axis_size("slab"), lax.axis_size("mem")
    members, rows, width = ensemble.shape
    place = lax.axis_index("mem").reshape(1)
    ens = ensemble.reshape(members, n_mem, rows // n_mem, width)
    coefs = jnp.concatenate([diffusivity[None], velocity], axis=0)
    up = [(i, (i + 1) % n_slab) for i in range(n_slab)]
    down = [(j, i) for i, j in up]

    def send(parts, sign):
        moved = [parts[0]]
        for shift in range(1, n_mem):
            ways = [(i, (i + sign * shift) % n_mem) for i in range(n_mem)]
            moved.append(lax.ppermute(parts[shift], "mem", ways))
        return moved

    head, tail = edges(ens, coefs)
    above = lax.ppermute(tail, "slab", up)
    below = lax.ppermute(head, "slab", down)
    early = send(forecast(0, n_mem, place, ens, coefs), 1)
    counts = tally(obs_value, obs_weight, obs_slab, obs_cell, n_slab, width)
    counts = counts.reshape(2, n_slab, SUB, width).transpose(1, 0, 2, 3)
    counts = lax.all_to_all(counts, "slab", split_axis=0, concat_axis=0, tiled=True)
    late = send(forecast(1, n_mem, place, ens, coefs, (above, below)), 1)
    early = send(analyse(0, n_mem, place, counts, early), -1)
    late = send(analyse(1, n_mem, place, counts, late), -1)
    return gather(n_mem, place, early, late).reshape(members, rows, width)


def solution(mesh):
    return jax.shard_map(
        shards,
        mesh=mesh,
        in_specs=(
            P("mem", "slab", None),
            P("slab", None),
            P(None, "slab", None),
            P(("mem", "slab")),
            P(("mem", "slab")),
            P(("mem", "slab"), None),
            P(("mem", "slab")),
        ),
        out_specs=P("mem", "slab", None),
        check_vma=False,
    )
```

time: 168 us -> 89.5 us (0.53)
  local copies, waits for them, and re-layouts: 52.9 us -> 4.83 us
  Pallas kernels: 0 us -> 42.4 us
  matrix products: 31 us -> 0 us
  blocking collectives: 27.9 us -> 0 us
  starting transfers between devices: 12.3 us -> 29.8 us
  other arithmetic: 19.4 us -> 1.99 us
  waiting for transfers between devices: 22.8 us -> 9.55 us
    pallas_call x0 -> x7, Pallas kernels: none -> 42.4 us  [the longest x2 24.3 us: forecast(): pl.pallas_call(functools.partial(forecast_kernel, chunk, n_mem), in_specs...]
    dot_general x25 -> x0, matrix products: 31 us -> none  [the longest x8 18.2 us: patch_gram(): jnp.einsum('mo,no->mn', weighted, at_obs, preferred_element_type=jnp.floa...]
    all_to_all x1 -> x0, blocking collectives: 27.9 us -> none  [shards(): lax.all_to_all(analysed, 'mem', split_axis=0, concat_axis=1, tiled=True)]
    ppermute x2 -> x14, starting transfers between devices: 3.36 us -> 26.4 us  [the longest x12 23.1 us: send(): moved.append(lax.ppermute(parts[shift], 'mem', ways))]
    all_to_all x2 -> x1, waiting for transfers between devices: 22.8 us -> 0.01 us  [shards(): lax.all_to_all(counts, 'slab', split_axis=0, concat_axis=0, tiled=True)]
    gather x2 -> x0, local copies, waits for them, and re-layouts: 17.5 us -> none  [the longest x1 9.38 us: analyse(): misfit = obs_vals - jnp.take(flat_mean, obs_cells)]
    ppermute x2 -> x14, waiting for transfers between devices: 0.01 us -> 9.55 us  [the longest x12 9.54 us: send(): moved.append(lax.ppermute(parts[shift], 'mem', ways))]
    all_to_all x4 -> x0, local copies, waits for them, and re-layouts: 7.72 us -> none  [the longest x3 6.61 us: shards(): lax.all_to_all(fields, 'mem', split_axis=1, concat_axis=0, tiled=True)]
  transfers between devices with their start and end apart: 4 -> 15, of which waited for: 1 -> 2; matrix products, arithmetic and copies ran while one was open for 15% -> 2% of each run, Pallas kernels for 0% -> 42%
where the time goes in v1:
time: 89.5 us; the launch traced here: 88.8 us
  Pallas kernels  42.4 us (47%)
  starting transfers between devices  29.8 us (33%)
  waiting for transfers between devices  9.55 us (11%)
  local copies, waits for them, and re-layouts  4.83 us (5%)
  other arithmetic  1.99 us (2%)
    pallas_call x2, Pallas kernels, forecast(): pl.pallas_call(functools.partial(forecast_kernel, chunk, n_mem), in_specs...  24.3 us
    ppermute x12, starting transfers between devices, send(): moved.append(lax.ppermute(parts[shift], 'mem', ways))  23.1 us
    pallas_call x2, Pallas kernels, analyse(): pl.pallas_call(functools.partial(analyse_kernel, chunk, n_mem), in_specs=...  10.5 us
    ppermute x12, waiting for transfers between devices, send(): moved.append(lax.ppermute(parts[shift], 'mem', ways))  9.54 us
    pallas_call x1, Pallas kernels, gather(): pl.pallas_call(functools.partial(gather_kernel, n_mem), grid=(local // bl...  3.63 us
    unnamed x32, local copies, waits for them, and re-layouts  3.35 us
    all_to_all x1, starting transfers between devices, shards(): lax.all_to_all(counts, 'slab', split_axis=0, concat_axis=0, tiled=True)  3.35 us
    ppermute x1, starting transfers between devices, shards(): below = lax.ppermute(head, 'slab', down)  2.87 us
  transfers between devices with their start and end apart: 15, of which 2 were waited for; matrix products, arithmetic and copies ran while one was open for 2% of the time, Pallas kernels for 42%

profile of v1, /device:TPU:0, one launch (start us, length us, event | category | flops | bytes accessed | tf_op | source)
XLA Modules:
  0.0 88.8 jit_solution(14424928045537044803)
XLA Ops:
  0.0 1.4 %pad_maximum_fusion.refs_2_.coef_ref = f32[3,32,128]{2,1,0:T(8,128)} fusion(f32[2,32,128]{2,1,0:T(8,128)} %param.9, f32[1,32,128]{2,1,0:T(8,128)} %bitcast.18), kind=kLoop, calls=%fused_computation.1 | loop fusion | flops 12288 | bytes 98304 | tf_op jit(solution)/shard_map/concatenate | solution.py:309
  1.4 1.9 %edges.1 = (f32[4,72,128]{2,1,0:T(8,128)}, f32[4,72,128]{2,1,0:T(8,128)}) custom-call(f32[64,4,8,128]{3,2,1,0:T(8,128)} %bitcast.13, f32[64,4,8,128]{3,2,1,0:T(8,128)} %bitcast.14, f32[3,32,128]{2,1,0:T(8,128)} %pad_maximum_fusion.refs_2_.coef_ref), custom_call_target="tpu_custom_call" | custom-call | tf_op jit(solution)/shard_map/edges/pallas_call | solution.py:39
  3.3 0.5 collective-permute-start.6
  3.8 2.9 %collective-permute-start.7 = (f32[4,72,128]{2,1,0:T(8,128)}, f32[4,72,128]{2,1,0:T(8,128)S(1)}, u32[]{:S(2)}, u32[]{:S(2)}) collective-permute-start(f32[4,72,128]{2,1,0:T(8,128)} %get-tuple-element.32), channel_id=1, source_target_pairs={{1,0},{2,1},{3,2},{4,3},{5,4},{6,5},{7,6},{0,7},{9,8},{10,9},{11,1... | collective-permute-start | bytes 442376 | tf_op jit(solution)/shard_map/ppermute | solution.py:322
  6.6 12.1 %forecast0.1 = (f32[4,64,128]{2,1,0:T(8,128)}, f32[4,64,128]{2,1,0:T(8,128)}, f32[4,64,128]{2,1,0:T(8,128)}, f32[4,64,128]{2,1,0:T(8,128)}) custom-call(s32[1]{0:T(128)} %bitcast.refs_0_.place, f32[64,4,8,128]{3,2,1,0:T(8,128)} %bitcast.15, f32[3,32,128]{2,1,0:T(8,128)} %pad_maximum_fusion.refs_2_.coef_ref), custom_call_target="tpu_custom_call" | custom-call | tf_op jit(solution)/shard_map/forecast0/pallas_call | solution.py:127
  18.7 0.0 copy-start.15
  18.7 2.3 %collective-permute-start = (f32[4,64,128]{2,1,0:T(8,128)}, f32[4,64,128]{2,1,0:T(8,128)S(1)}, u32[]{:S(2)}, u32[]{:S(2)}) collective-permute-start(f32[4,64,128]{2,1,0:T(8,128)} %get-tuple-element.24), channel_id=1, source_target_pairs={{0,8},{8,16},{16,24},{24,0},{1,9},{9,17},{17,25},{25,1},{2,10},{10... | collective-permute-start | bytes 393224 | tf_op jit(solution)/shard_map/ppermute | solution.py:317
  21.0 2.6 %collective-permute-start.1 = (f32[4,64,128]{2,1,0:T(8,128)}, f32[4,64,128]{2,1,0:T(8,128)S(1)}, u32[]{:S(2)}, u32[]{:S(2)}) collective-permute-start(f32[4,64,128]{2,1,0:T(8,128)} %get-tuple-element.25), channel_id=1, source_target_pairs={{0,16},{8,24},{16,0},{24,8},{1,17},{9,25},{17,1},{25,9},{2,18},{10... | collective-permute-start | bytes 393224 | tf_op jit(solution)/shard_map/ppermute | solution.py:317
  23.6 1.3 %collective-permute-start.2 = (f32[4,64,128]{2,1,0:T(8,128)}, f32[4,64,128]{2,1,0:T(8,128)S(1)}, u32[]{:S(2)}, u32[]{:S(2)}) collective-permute-start(f32[4,64,128]{2,1,0:T(8,128)} %get-tuple-element.26), channel_id=1, source_target_pairs={{0,24},{8,0},{16,8},{24,16},{1,25},{9,1},{17,9},{25,17},{2,26},{10... | collective-permute-start | bytes 393224 | tf_op jit(solution)/shard_map/ppermute | solution.py:317
  25.0 0.0 copy-done.15
  25.0 0.6 reduce
  25.6 2.2 %tally.1 = f32[2,64,128]{2,1,0:T(8,128)} custom-call(f32[10,128]{1,0:T(8,128)} %bitcast.19, f32[10,128]{1,0:T(8,128)} %bitcast.20, s32[10,128]{1,0:T(8,128)} %bitcast.17, s32[10,128]{1,0:T(8,128)} %bitcast.21), custom_call_target="tpu_custom_call" | custom-call | tf_op jit(solution)/shard_map/tally/pallas_call | solution.py:169
  27.8 1.5 %copy_bitcast_fusion = f32[8,2,8,128]{3,2,1,0:T(8,128)} fusion(f32[2,64,128]{2,1,0:T(8,128)} %tally.1), kind=kLoop, calls=%fused_computation | loop fusion | bytes 131072 | tf_op jit(solution)/shard_map/transpose | solution.py:325
  29.2 3.3 %all-to-all-start = ((f32[8,2,8,128]{3,2,1,0:T(8,128)}), f32[8,2,8,128]{3,2,1,0:T(8,128)S(1)}, u32[]{:S(2)}, u32[]{:S(2)}) async-start(f32[8,2,8,128]{3,2,1,0:T(8,128)} %copy_bitcast_fusion), calls=%async_computation | async-start | bytes 131072 | tf_op jit(solution)/shard_map/all_to_all | solution.py:326
  32.6 0.0 collective-permute-done.6.refs_3_
  32.6 0.0 copy-start.1
  32.6 0.0 collective-permute-done.7.refs_4_
  32.6 0.6 copy-done.1
  33.3 0.0 copy-start.2
  33.3 0.7 copy-done.2
  33.9 12.2 %forecast1.1 = (f32[4,64,128]{2,1,0:T(8,128)}, f32[4,64,128]{2,1,0:T(8,128)}, f32[4,64,128]{2,1,0:T(8,128)}, f32[4,64,128]{2,1,0:T(8,128)}) custom-call(s32[1]{0:T(128)} %bitcast.refs_0_.place, f32[64,4,8,128]{3,2,1,0:T(8,128)} %bitcast.16, f32[3,32,128]{2,1,0:T(8,128)} %pad_maximum_fusion.refs_2_.coef_ref, f32[4,72,128]{2,1,0:T(8,128)} %copy-done.1, ...), custom_call_target="tpu_custom_call" | custom-call | tf_op jit(solution)/shard_map/forecast1/pallas_call | solution.py:127
  46.1 0.7 collective-permute-start.8
  46.8 0.3 collective-permute-start.9
  47.2 0.0 collective-permute-done.refs_1_
  47.2 0.0 copy-start.9
  47.2 2.9 %collective-permute-start.10 = (f32[4,64,128]{2,1,0:T(8,128)}, f32[4,64,128]{2,1,0:T(8,128)S(1)}, u32[]{:S(2)}, u32[]{:S(2)}) collective-permute-start(f32[4,64,128]{2,1,0:T(8,128)} %get-tuple-element.36), channel_id=1, source_target_pairs={{0,24},{8,0},{16,8},{24,16},{1,25},{9,1},{17,9},{25,17},{2,26},{10... | collective-permute-start | bytes 393224 | tf_op jit(solution)/shard_map/ppermute | solution.py:317
  50.0 0.0 all-to-all-done.tallies_ref
  50.0 0.0 collective-permute-done.1.refs_2_
  50.0 0.0 copy-start.10
  50.0 0.0 collective-permute-done.2.refs_3_
  50.1 0.0 copy-start.12
  50.1 0.0 copy-done.9
  50.1 0.6 copy-done
  50.6 0.0 copy-done.10
  50.7 0.1 copy-done.12
  50.8 5.2 %analyse0.1 = (f32[4,64,128]{2,1,0:T(8,128)}, f32[4,64,128]{2,1,0:T(8,128)}, f32[4,64,128]{2,1,0:T(8,128)}, f32[4,64,128]{2,1,0:T(8,128)}) custom-call(s32[1]{0:T(128)} %bitcast.refs_0_.place, f32[8,2,8,128]{3,2,1,0:T(8,128)} %copy-done, f32[4,64,128]{2,1,0:T(8,128)} %get-tuple-element.23.refs_0_, f32[4,64,128]{2,1,0:T(8,128)} %copy-done.9, ...), custom_call_target="tpu_custom_call" | custom-call | tf_op jit(solution)/shard_map/analyse0/pallas_call | solution.py:270
  56.0 1.2 %collective-permute-start.3 = (f32[4,64,128]{2,1,0:T(8,128)}, f32[4,64,128]{2,1,0:T(8,128)S(1)}, u32[]{:S(2)}, u32[]{:S(2)}) collective-permute-start(f32[4,64,128]{2,1,0:T(8,128)} %get-tuple-element.28), channel_id=1, source_target_pairs={{0,24},{8,0},{16,8},{24,16},{1,25},{9,1},{17,9},{25,17},{2,26},{10... | collective-permute-start | bytes 393224 | tf_op jit(solution)/shard_map/ppermute | solution.py:317
  57.2 0.8 collective-permute-start.4
  58.0 0.0 collective-permute-done.8.refs_1_
  58.0 2.0 %collective-permute-start.5 = (f32[4,64,128]{2,1,0:T(8,128)}, f32[4,64,128]{2,1,0:T(8,128)S(1)}, u32[]{:S(2)}, u32[]{:S(2)}) collective-permute-start(f32[4,64,128]{2,1,0:T(8,128)} %get-tuple-element.30), channel_id=1, source_target_pairs={{0,8},{8,16},{16,24},{24,0},{1,9},{9,17},{17,25},{25,1},{2,10},{10... | collective-permute-start | bytes 393224 | tf_op jit(solution)/shard_map/ppermute | solution.py:317
  60.0 0.0 collective-permute-done.9.refs_2_
  60.0 0.0 collective-permute-done.10.refs_3_
  60.0 0.0 copy-start.14
  60.0 0.0 copy-done.11
  60.0 0.6 copy-done.13
  60.6 0.1 copy-done.14
  60.7 5.2 %analyse1.1 = (f32[4,64,128]{2,1,0:T(8,128)}, f32[4,64,128]{2,1,0:T(8,128)}, f32[4,64,128]{2,1,0:T(8,128)}, f32[4,64,128]{2,1,0:T(8,128)}) custom-call(s32[1]{0:T(128)} %bitcast.refs_0_.place, f32[8,2,8,128]{3,2,1,0:T(8,128)} %copy-done, f32[4,64,128]{2,1,0:T(8,128)} %get-tuple-element.33.refs_0_, f32[4,64,128]{2,1,0:T(8,128)} %copy-done.11, ...), custom_call_target="tpu_custom_call" | custom-call | tf_op jit(solution)/shard_map/analyse1/pallas_call | solution.py:270
  66.0 8.4 %collective-permute-start.11 = (f32[4,64,128]{2,1,0:T(8,128)}, f32[4,64,128]{2,1,0:T(8,128)S(1)}, u32[]{:S(2)}, u32[]{:S(2)}) collective-permute-start(f32[4,64,128]{2,1,0:T(8,128)} %get-tuple-element.38), channel_id=1, source_target_pairs={{0,24},{8,0},{16,8},{24,16},{1,25},{9,1},{17,9},{25,17},{2,26},{10... | collective-permute-start | bytes 393224 | tf_op jit(solution)/shard_map/ppermute | solution.py:317
  74.3 0.0 collective-permute-start.12
  74.3 0.0 collective-permute-done.3.refs_1_
  74.3 0.6 collective-permute-start.13
  74.9 0.0 collective-permute-done.4.refs_2_
  74.9 0.0 collective-permute-done.5.refs_3_
  74.9 0.0 copy-start.5
  74.9 3.4 %collective-permute-done.11.refs_5_ = f32[4,64,128]{2,1,0:T(8,128)S(1)} collective-permute-done((f32[4,64,128]{2,1,0:T(8,128)}, f32[4,64,128]{2,1,0:T(8,128)S(1)}, u32[]{:S(2)}, u32[]{:S(2)}) %collective-permute-start.11) | collective-permute-done | bytes 131104 | tf_op jit(solution)/shard_map/ppermute | solution.py:317
  78.3 6.1 %collective-permute-done.12.refs_6_ = f32[4,64,128]{2,1,0:T(8,128)S(1)} collective-permute-done((f32[4,64,128]{2,1,0:T(8,128)}, f32[4,64,128]{2,1,0:T(8,128)S(1)}, u32[]{:S(2)}, u32[]{:S(2)}) %collective-permute-start.12) | collective-permute-done | bytes 131104 | tf_op jit(solution)/shard_map/ppermute | solution.py:317
  84.4 0.0 collective-permute-done.13.refs_7_
  84.4 0.0 copy-done.3
  84.5 0.0 copy-done.4
  84.5 0.0 copy-done.5
  84.5 0.0 copy-done.6
  84.5 0.6 copy-done.7
  85.1 0.0 copy-done.8
  85.1 3.6 %gather.1 = f32[64,4,8,128]{3,2,1,0:T(8,128)} custom-call(s32[1]{0:T(128)} %bitcast.refs_0_.place, f32[4,64,128]{2,1,0:T(8,128)} %get-tuple-element.27.refs_0_, f32[4,64,128]{2,1,0:T(8,128)} %copy-done.3, f32[4,64,128]{2,1,0:T(8,128)} %copy-done.4, f32[4,64,128]{2,1,0:T(8,128)} %copy-done.5, f32[4,64,128]{2,1,0:T(8,128)} %get-tuple-element.37.refs_4_, ...), custom_call_target="tpu_custom_call" | custom-call | tf_op jit(solution)/shard_map/gather/pallas_call | solution.py:294
  (8 shorter events, 0.0 us)
Async XLA Ops:
  3.3 29.3 %collective-permute-start.6 = (f32[4,72,128]{2,1,0:T(8,128)}, f32[4,72,128]{2,1,0:T(8,128)S(1)}, u32[]{:S(2)}, u32[]{:S(2)}) collective-permute-start(f32[4,72,128]{2,1,0:T(8,128)} %get-tuple-element.31), channel_id=1, source_target_pairs={{0,1},{1,2},{2,3},{3,4},{4,5},{5,6},{6,7},{7,0},{8,9},{9,10},{10,1... | collective-permute-start | bytes 442376 | tf_op jit(solution)/shard_map/ppermute | solution.py:321
  3.8 28.9 %collective-permute-start.7 = (f32[4,72,128]{2,1,0:T(8,128)}, f32[4,72,128]{2,1,0:T(8,128)S(1)}, u32[]{:S(2)}, u32[]{:S(2)}) collective-permute-start(f32[4,72,128]{2,1,0:T(8,128)} %get-tuple-element.32), channel_id=1, source_target_pairs={{1,0},{2,1},{3,2},{4,3},{5,4},{6,5},{7,6},{0,7},{9,8},{10,9},{11,1... | collective-permute-start | bytes 442376 | tf_op jit(solution)/shard_map/ppermute | solution.py:322
  18.7 6.3 %copy-start.15 = (s32[1280,1]{0,1:T(1,128)S(1)}, s32[1280,1]{0,1:T(1,128)}, u32[]{:S(2)}) copy-start(s32[1280,1]{0,1:T(1,128)} %param.12) | copy-start | bytes 15364
  18.7 28.4 %collective-permute-start = (f32[4,64,128]{2,1,0:T(8,128)}, f32[4,64,128]{2,1,0:T(8,128)S(1)}, u32[]{:S(2)}, u32[]{:S(2)}) collective-permute-start(f32[4,64,128]{2,1,0:T(8,128)} %get-tuple-element.24), channel_id=1, source_target_pairs={{0,8},{8,16},{16,24},{24,0},{1,9},{9,17},{17,25},{25,1},{2,10},{10... | collective-permute-start | bytes 393224 | tf_op jit(solution)/shard_map/ppermute | solution.py:317
  21.0 29.0 %collective-permute-start.1 = (f32[4,64,128]{2,1,0:T(8,128)}, f32[4,64,128]{2,1,0:T(8,128)S(1)}, u32[]{:S(2)}, u32[]{:S(2)}) collective-permute-start(f32[4,64,128]{2,1,0:T(8,128)} %get-tuple-element.25), channel_id=1, source_target_pairs={{0,16},{8,24},{16,0},{24,8},{1,17},{9,25},{17,1},{25,9},{2,18},{10... | collective-permute-start | bytes 393224 | tf_op jit(solution)/shard_map/ppermute | solution.py:317
  23.6 26.4 %collective-permute-start.2 = (f32[4,64,128]{2,1,0:T(8,128)}, f32[4,64,128]{2,1,0:T(8,128)S(1)}, u32[]{:S(2)}, u32[]{:S(2)}) collective-permute-start(f32[4,64,128]{2,1,0:T(8,128)} %get-tuple-element.26), channel_id=1, source_target_pairs={{0,24},{8,0},{16,8},{24,16},{1,25},{9,1},{17,9},{25,17},{2,26},{10... | collective-permute-start | bytes 393224 | tf_op jit(solution)/shard_map/ppermute | solution.py:317
  29.2 20.8 %all-to-all-start = ((f32[8,2,8,128]{3,2,1,0:T(8,128)}), f32[8,2,8,128]{3,2,1,0:T(8,128)S(1)}, u32[]{:S(2)}, u32[]{:S(2)}) async-start(f32[8,2,8,128]{3,2,1,0:T(8,128)} %copy_bitcast_fusion), calls=%async_computation | async-start | bytes 131072 | tf_op jit(solution)/shard_map/all_to_all | solution.py:326
  32.6 0.7 copy-start.1
  33.3 0.7 copy-start.2
  46.1 11.9 %collective-permute-start.8 = (f32[4,64,128]{2,1,0:T(8,128)}, f32[4,64,128]{2,1,0:T(8,128)S(1)}, u32[]{:S(2)}, u32[]{:S(2)}) collective-permute-start(f32[4,64,128]{2,1,0:T(8,128)} %get-tuple-element.34), channel_id=1, source_target_pairs={{0,8},{8,16},{16,24},{24,0},{1,9},{9,17},{17,25},{25,1},{2,10},{10... | collective-permute-start | bytes 393224 | tf_op jit(solution)/shard_map/ppermute | solution.py:317
  46.8 13.2 %collective-permute-start.9 = (f32[4,64,128]{2,1,0:T(8,128)}, f32[4,64,128]{2,1,0:T(8,128)S(1)}, u32[]{:S(2)}, u32[]{:S(2)}) collective-permute-start(f32[4,64,128]{2,1,0:T(8,128)} %get-tuple-element.35), channel_id=1, source_target_pairs={{0,16},{8,24},{16,0},{24,8},{1,17},{9,25},{17,1},{25,9},{2,18},{10... | collective-permute-start | bytes 393224 | tf_op jit(solution)/shard_map/ppermute | solution.py:317
  47.2 2.9 %copy-start.9 = (f32[4,64,128]{2,1,0:T(8,128)}, f32[4,64,128]{2,1,0:T(8,128)S(1)}, u32[]{:S(2)}) copy-start(f32[4,64,128]{2,1,0:T(8,128)S(1)} %collective-permute-done.refs_1_) | copy-start | bytes 393220
  47.2 12.9 %collective-permute-start.10 = (f32[4,64,128]{2,1,0:T(8,128)}, f32[4,64,128]{2,1,0:T(8,128)S(1)}, u32[]{:S(2)}, u32[]{:S(2)}) collective-permute-start(f32[4,64,128]{2,1,0:T(8,128)} %get-tuple-element.36), channel_id=1, source_target_pairs={{0,24},{8,0},{16,8},{24,16},{1,25},{9,1},{17,9},{25,17},{2,26},{10... | collective-permute-start | bytes 393224 | tf_op jit(solution)/shard_map/ppermute | solution.py:317
  50.0 0.6 copy-start
  50.0 0.7 copy-start.10
  50.1 0.7 copy-start.12
  56.0 18.3 %collective-permute-start.3 = (f32[4,64,128]{2,1,0:T(8,128)}, f32[4,64,128]{2,1,0:T(8,128)S(1)}, u32[]{:S(2)}, u32[]{:S(2)}) collective-permute-start(f32[4,64,128]{2,1,0:T(8,128)} %get-tuple-element.28), channel_id=1, source_target_pairs={{0,24},{8,0},{16,8},{24,16},{1,25},{9,1},{17,9},{25,17},{2,26},{10... | collective-permute-start | bytes 393224 | tf_op jit(solution)/shard_map/ppermute | solution.py:317
  57.2 17.7 %collective-permute-start.4 = (f32[4,64,128]{2,1,0:T(8,128)}, f32[4,64,128]{2,1,0:T(8,128)S(1)}, u32[]{:S(2)}, u32[]{:S(2)}) collective-permute-start(f32[4,64,128]{2,1,0:T(8,128)} %get-tuple-element.29), channel_id=1, source_target_pairs={{0,16},{8,24},{16,0},{24,8},{1,17},{9,25},{17,1},{25,9},{2,18},{10... | collective-permute-start | bytes 393224 | tf_op jit(solution)/shard_map/ppermute | solution.py:317
  58.0 2.0 %copy-start.11 = (f32[4,64,128]{2,1,0:T(8,128)}, f32[4,64,128]{2,1,0:T(8,128)S(1)}, u32[]{:S(2)}) copy-start(f32[4,64,128]{2,1,0:T(8,128)S(1)} %collective-permute-done.8.refs_1_) | copy-start | bytes 393220
  58.0 16.9 %collective-permute-start.5 = (f32[4,64,128]{2,1,0:T(8,128)}, f32[4,64,128]{2,1,0:T(8,128)S(1)}, u32[]{:S(2)}, u32[]{:S(2)}) collective-permute-start(f32[4,64,128]{2,1,0:T(8,128)} %get-tuple-element.30), channel_id=1, source_target_pairs={{0,8},{8,16},{16,24},{24,0},{1,9},{9,17},{17,25},{25,1},{2,10},{10... | collective-permute-start | bytes 393224 | tf_op jit(solution)/shard_map/ppermute | solution.py:317
  60.0 0.6 copy-start.13
  60.0 0.7 copy-start.14
  66.0 12.3 %collective-permute-start.11 = (f32[4,64,128]{2,1,0:T(8,128)}, f32[4,64,128]{2,1,0:T(8,128)S(1)}, u32[]{:S(2)}, u32[]{:S(2)}) collective-permute-start(f32[4,64,128]{2,1,0:T(8,128)} %get-tuple-element.38), channel_id=1, source_target_pairs={{0,24},{8,0},{16,8},{24,16},{1,25},{9,1},{17,9},{25,17},{2,26},{10... | collective-permute-start | bytes 393224 | tf_op jit(solution)/shard_map/ppermute | solution.py:317
  74.3 10.1 %collective-permute-start.12 = (f32[4,64,128]{2,1,0:T(8,128)}, f32[4,64,128]{2,1,0:T(8,128)S(1)}, u32[]{:S(2)}, u32[]{:S(2)}) collective-permute-start(f32[4,64,128]{2,1,0:T(8,128)} %get-tuple-element.39), channel_id=1, source_target_pairs={{0,16},{8,24},{16,0},{24,8},{1,17},{9,25},{17,1},{25,9},{2,18},{10... | collective-permute-start | bytes 393224 | tf_op jit(solution)/shard_map/ppermute | solution.py:317
  74.3 10.1 %copy-start.3 = (f32[4,64,128]{2,1,0:T(8,128)}, f32[4,64,128]{2,1,0:T(8,128)S(1)}, u32[]{:S(2)}) copy-start(f32[4,64,128]{2,1,0:T(8,128)S(1)} %collective-permute-done.3.refs_1_) | copy-start | bytes 393220
  74.3 10.1 %collective-permute-start.13 = (f32[4,64,128]{2,1,0:T(8,128)}, f32[4,64,128]{2,1,0:T(8,128)S(1)}, u32[]{:S(2)}, u32[]{:S(2)}) collective-permute-start(f32[4,64,128]{2,1,0:T(8,128)} %get-tuple-element.40), channel_id=1, source_target_pairs={{0,8},{8,16},{16,24},{24,0},{1,9},{9,17},{17,25},{25,1},{2,10},{10... | collective-permute-start | bytes 393224 | tf_op jit(solution)/shard_map/ppermute | solution.py:317
  74.9 9.6 %copy-start.4 = (f32[4,64,128]{2,1,0:T(8,128)}, f32[4,64,128]{2,1,0:T(8,128)S(1)}, u32[]{:S(2)}) copy-start(f32[4,64,128]{2,1,0:T(8,128)S(1)} %collective-permute-done.4.refs_2_) | copy-start | bytes 393220
  74.9 9.6 %copy-start.5 = (f32[4,64,128]{2,1,0:T(8,128)}, f32[4,64,128]{2,1,0:T(8,128)S(1)}, u32[]{:S(2)}) copy-start(f32[4,64,128]{2,1,0:T(8,128)S(1)} %collective-permute-done.5.refs_3_) | copy-start | bytes 393220
  78.3 6.2 %copy-start.6 = (f32[4,64,128]{2,1,0:T(8,128)}, f32[4,64,128]{2,1,0:T(8,128)S(1)}, u32[]{:S(2)}) copy-start(f32[4,64,128]{2,1,0:T(8,128)S(1)} %collective-permute-done.11.refs_5_) | copy-start | bytes 393220
  84.4 0.6 copy-start.7
  84.4 0.7 copy-start.8

commit v2 on v1

--- a/solution.py
+++ b/solution.py
@@ -18,55 +18,20 @@
 SMEM = pl.BlockSpec(memory_space=pltpu.SMEM)
 
 
-def edge_kernel(top_ref, bottom_ref, coef_ref, head_ref, tail_ref):
-    members = top_ref.shape[0]
-    rows = coef_ref.shape[1]
-    for r in range(STEPS):
-        head_ref[r, :members, :] = top_ref[:, 0, r, :]
-        tail_ref[r, :members, :] = bottom_ref[:, 0, SUB - STEPS + r, :]
-        for k in range(3):
-            head_ref[r, members + k : members + k + 1, :] = coef_ref[k, r : r + 1, :]
-            tail_ref[r, members + k : members + k + 1, :] = coef_ref[
-                k, rows - STEPS + r : rows - STEPS + r + 1, :
-            ]
-
-
-def edges(ens, coefs):
-    members, groups = ens.shape[:2]
-    width = ens.shape[-1]
-    shape = jax.ShapeDtypeStruct((STEPS, members + SUB, width), F32)
-    block = (members, 1, SUB, width)
-    return pl.pallas_call(
-        edge_kernel,
-        grid=(1,),
-        in_specs=[
-            pl.BlockSpec(block, lambda i: (0, 0, 0, 0)),
-            pl.BlockSpec(block, lambda i: (0, groups - 1, 0, 0)),
-            pl.BlockSpec(coefs.shape, lambda i: (0, 0, 0)),
-        ],
-        out_specs=[pl.BlockSpec(shape.shape, lambda i: (0, 0, 0))] * 2,
-        out_shape=[shape] * 2,
-        name="edges",
-    )(ens, ens, coefs)
-
-
 def forecast_kernel(chunk, n_mem, *refs):
+    place, ens_ref, diffuse_ref, drift_ref = refs[:4]
     if chunk:
-        place, ens_ref, coef_ref, above_ref, below_ref = refs[:5]
-        refs = refs[5:]
+        halos, refs = ((0, refs[4]), (1, refs[5])), refs[6:]
     else:
-        place, ens_ref, coef_ref = refs[:3]
-        refs = refs[3:]
-    outs, field, table = refs[:n_mem], refs[n_mem], refs[n_mem + 1]
-    members, groups, _, width = ens_ref.shape
-    rows = groups * SUB
-
-    for g in range(groups):
-        for r in range(SUB):
-            field[STEPS + g * SUB + r] = ens_ref[:, g, r, :]
-
-    def put_table(first, diffuse, drift_x, drift_y):
-        count = diffuse.shape[0]
+        edges, refs = refs[4:6], refs[6:]
+    outs, (field, table, ping, pong) = refs[:n_mem], refs[n_mem:]
+    rows, width = diffuse_ref.shape
+    members = ens_ref.shape[0] // rows
+
+    for r in range(rows):
+        field[STEPS + r] = ens_ref[pl.ds(r, members, stride=rows), :]
+
+    def put_table(row, diffuse, drift_x, drift_y):
         parts = (
             1.0 - 4.0 * diffuse,
             diffuse - 0.5 * drift_x,
@@ -74,21 +39,25 @@
             diffuse + 0.5 * drift_y,
             diffuse - 0.5 * drift_y,
         )
-        for r in range(count):
-            for k, part in enumerate(parts):
-                table[first + r, k] = jnp.broadcast_to(part[r : r + 1], (SUB, width))
-
-    put_table(STEPS, coef_ref[0], coef_ref[1], coef_ref[2])
+        for k, part in enumerate(parts):
+            for r in range(part.shape[0]):
+                table[row + r, k] = jnp.broadcast_to(part[r : r + 1], (SUB, width))
+
+    put_table(STEPS, diffuse_ref[...], drift_ref[0], drift_ref[1])
     if chunk:
-        for first, edge in ((0, above_ref), (STEPS + rows, below_ref)):
+        for below, halo in halos:
             for r in range(STEPS):
-                field[first + r] = edge[r, :members, :]
-                put_table(
-                    first + r,
-                    edge[r, members : members + 1, :],
-                    edge[r, members + 1 : members + 2, :],
-                    edge[r, members + 2 : members + 3, :],
-                )
+                row = r + below * (STEPS + rows)
+                field[row] = halo[r, :members, :]
+                put_table(row, *(halo[r, members + k : members + k + 1, :] for k in range(3)))
+    else:
+        for edge, first in zip(edges, (0, rows - STEPS)):
+            for r in range(STEPS):
+                row = first + r
+                edge[r, :members, :] = field[STEPS + row]
+                edge[r, members : members + 1, :] = diffuse_ref[row : row + 1, :]
+                for k in range(2):
+                    edge[r, members + 1 + k : members + 2 + k, :] = drift_ref[k, row : row + 1, :]
 
     for shift in range(n_mem):
         group = lax.rem(place[0] + shift, n_mem)
@@ -96,51 +65,48 @@
             start = jnp.where(group == 0, 0, group * SUB + STEPS)
         else:
             start = jnp.where(group == 0, STEPS, group * SUB)
-
-        def some_members(b, carry, start=start, out=outs[shift]):
-            at = pl.ds(pl.multiple_of(b * SUB, SUB), SUB)
-            now = [field[start + i, at, :] for i in range(HALF + 2 * STEPS)]
-            for step in range(STEPS):
-                after = []
-                for i in range(1, len(now) - 1):
-                    row = start + step + i
-                    center = now[i]
-                    east = pltpu.roll(center, width - 1, 1)
-                    west = pltpu.roll(center, 1, 1)
-                    after.append(
-                        (center * table[row, 0] + east * table[row, 1])
-                        + (west * table[row, 2] + now[i - 1] * table[row, 3])
-                        + now[i + 1] * table[row, 4]
+        for step in range(STEPS):
+            source = field.at[pl.ds(start, HALF + 2 * STEPS)] if step == 0 else (pong, ping)[step % 2]
+            target = outs[shift] if step == STEPS - 1 else (ping, pong)[step % 2]
+            for i in range(HALF + 2 * (STEPS - 1 - step)):
+                coef = [table[start + step + 1 + i, k] for k in range(5)]
+                for m in range(0, members, SUB):
+                    at = pl.ds(m, SUB)
+                    center = source[i + 1, at, :]
+                    target[i, at, :] = (
+                        (center * coef[0] + pltpu.roll(center, width - 1, 1) * coef[1])
+                        + (pltpu.roll(center, 1, 1) * coef[2] + source[i, at, :] * coef[3])
+                        + source[i + 2, at, :] * coef[4]
                     )
-                now = after
-            for i in range(HALF):
-                out[i, at, :] = now[i]
-            return carry
-
-        lax.fori_loop(0, members // SUB, some_members, 0)
-
-
-def forecast(chunk, n_mem, place, ens, coefs, halos=()):
-    members, groups, _, width = ens.shape
-    rows = groups * SUB
-    shape = jax.ShapeDtypeStruct((HALF, members, width), F32)
-    return pl.pallas_call(
+
+
+def forecast(chunk, n_mem, place, ens, diffusivity, velocity, halos=()):
+    rows, width = diffusivity.shape
+    members = ens.shape[0] // rows
+    part = jax.ShapeDtypeStruct((HALF, members, width), F32)
+    edge = jax.ShapeDtypeStruct((STEPS, members + SUB, width), F32)
+    shapes = ([] if chunk else [edge] * 2) + [part] * n_mem
+    outs = pl.pallas_call(
         functools.partial(forecast_kernel, chunk, n_mem),
-        in_specs=[SMEM] + [VMEM] * (2 + len(halos)),
-        out_specs=[VMEM] * n_mem,
-        out_shape=[shape] * n_mem,
+        in_specs=[SMEM] + [VMEM] * (3 + len(halos)),
+        out_specs=[VMEM] * len(shapes),
+        out_shape=shapes,
         scratch_shapes=[
             pltpu.VMEM((rows + 2 * STEPS, members, width), F32),
             pltpu.VMEM((rows + 2 * STEPS, 5, SUB, width), F32),
+            pltpu.VMEM((HALF + 2 * STEPS, members, width), F32),
+            pltpu.VMEM((HALF + 2 * STEPS, members, width), F32),
         ],
         name=f"forecast{chunk}",
-    )(place, ens, coefs, *halos)
+    )(place, ens, diffusivity, velocity, *halos)
+    return outs[: len(outs) - n_mem], outs[len(outs) - n_mem :]
 
 
 def tally_kernel(value_ref, weight_ref, slab_ref, cell_ref, out_ref):
     blocks, lanes = value_ref.shape
-    bins = out_ref.shape[1]
-    width = out_ref.shape[2]
+    n_slab = out_ref.shape[0]
+    width = out_ref.shape[-1]
+    bins = n_slab * SUB
     bin_id = lax.broadcasted_iota(jnp.int32, (bins, lanes), 0)
     column_id = lax.broadcasted_iota(jnp.int32, (width, lanes), 0)
     totals = jnp.zeros((2 * bins, width), F32)
@@ -160,8 +126,8 @@
             totals = totals + lax.dot_general(
                 piece, column, (((1,), (1,)), ((), ())), preferred_element_type=F32
             )
-    out_ref[0] = totals[:bins]
-    out_ref[1] = totals[bins:]
+    for k in range(2 * n_slab):
+        out_ref[k % n_slab, k // n_slab] = totals[k * SUB : (k + 1) * SUB]
 
 
 def tally(value, weight, slab, cell, n_slab, width):
@@ -170,7 +136,7 @@
         tally_kernel,
         in_specs=[VMEM] * 4,
         out_specs=VMEM,
-        out_shape=jax.ShapeDtypeStruct((2, n_slab * SUB, width), F32),
+        out_shape=jax.ShapeDtypeStruct((n_slab, 2, SUB, width), F32),
         name="tally",
     )(*(a.reshape(-1, lanes) for a in (value, weight, slab, cell)))
 
@@ -279,24 +245,29 @@
 
 def gather_kernel(n_mem, place, *refs):
     early, late, out_ref = refs[:n_mem], refs[n_mem : 2 * n_mem], refs[2 * n_mem]
+    rows = n_mem * SUB
+    members = out_ref.shape[0] // rows
     for shift in range(n_mem):
         group = lax.rem(place[0] + shift, n_mem)
+        first = group == 0
         for r in range(HALF):
             a, b = early[shift][r], late[shift][r]
-            out_ref[:, group, r, :] = jnp.where(group == 0, b, a)
-            out_ref[:, group, HALF + r, :] = jnp.where(group == 0, a, b)
+            start = group * SUB + r
+            out_ref[pl.ds(start, members, stride=rows), :] = jnp.where(first, b, a)
+            out_ref[pl.ds(start + HALF, members, stride=rows), :] = jnp.where(first, a, b)
 
 
 def gather(n_mem, place, early, late):
     local, width = early[0].shape[1:]
     block = min(local, 2 * SUB)
+    rows = n_mem * SUB
     part = pl.BlockSpec((HALF, block, width), lambda i: (0, i, 0))
     return pl.pallas_call(
         functools.partial(gather_kernel, n_mem),
         grid=(local // block,),
         in_specs=[SMEM] + [part] * (2 * n_mem),
-        out_specs=pl.BlockSpec((block, n_mem, SUB, width), lambda i: (i, 0, 0, 0)),
-        out_shape=jax.ShapeDtypeStruct((local, n_mem, SUB, width), F32),
+        out_specs=pl.BlockSpec((block * rows, width), lambda i: (i, 0)),
+        out_shape=jax.ShapeDtypeStruct((local * rows, width), F32),
         name="gather",
     )(place, *early, *late)
 
@@ -305,8 +276,8 @@
     n_slab, n_mem = lax.axis_size("slab"), lax.axis_size("mem")
     members, rows, width = ensemble.shape
     place = lax.axis_index("mem").reshape(1)
-    ens = ensemble.reshape(members, n_mem, rows // n_mem, width)
-    coefs = jnp.concatenate([diffusivity[None], velocity], axis=0)
+    ens = ensemble.reshape(members * rows, width)
+    assert rows == n_mem * SUB
     up = [(i, (i + 1) % n_slab) for i in range(n_slab)]
     down = [(j, i) for i, j in up]
 
@@ -317,14 +288,14 @@
             moved.append(lax.ppermute(parts[shift], "mem", ways))
         return moved
 
-    head, tail = edges(ens, coefs)
+    (head, tail), early = forecast(0, n_mem, place, ens, diffusivity, velocity)
     above = lax.ppermute(tail, "slab", up)
     below = lax.ppermute(head, "slab", down)
-    early = send(forecast(0, n_mem, place, ens, coefs), 1)
+    early = send(early, 1)
     counts = tally(obs_value, obs_weight, obs_slab, obs_cell, n_slab, width)
-    counts = counts.reshape(2, n_slab, SUB, width).transpose(1, 0, 2, 3)
     counts = lax.all_to_all(counts, "slab", split_axis=0, concat_axis=0, tiled=True)
-    late = send(forecast(1, n_mem, place, ens, coefs, (above, below)), 1)
+    _, late = forecast(1, n_mem, place, ens, diffusivity, velocity, (above, below))
+    late = send(late, 1)
     early = send(analyse(0, n_mem, place, counts, early), -1)
     late = send(analyse(1, n_mem, place, counts, late), -1)
     return gather(n_mem, place, early, late).reshape(members, rows, width)

time: 89.5 us -> 69.4 us (0.78)
  Pallas kernels: 42.4 us -> 25.4 us
  local copies, waits for them, and re-layouts: 4.83 us -> 3.37 us
  other arithmetic: 1.99 us -> 0.62 us
    pallas_call x2, Pallas kernels: 24.3 us -> 9.08 us  [forecast(): pl.pallas_call(functools.partial(forecast_kernel, chunk, n_mem), in_specs...]
    pallas_call x1 -> x0, Pallas kernels: 1.88 us -> none  [edges(): pl.pallas_call(edge_kernel, grid=(1,), in_specs=[pl.BlockSpec(block, lamb...]
    transpose x1 -> x0, local copies, waits for them, and re-layouts: 1.48 us -> none  [shards(): counts = counts.reshape(2, n_slab, SUB, width).transpose(1, 0, 2, 3)]
    concatenate x1 -> x0, other arithmetic: 1.38 us -> none  [shards(): coefs = jnp.concatenate([diffusivity[None], velocity], axis=0)]
  transfers between devices with their start and end apart: 15 -> 15, of which waited for: 2 -> 2; matrix products, arithmetic and copies ran while one was open for 2% -> 1% of each run, Pallas kernels for 42% -> 25%
where the time goes in v2:
time: 69.4 us; the launch traced here: 68.9 us
  starting transfers between devices  29.8 us (43%)
  Pallas kernels  25.4 us (37%)
  waiting for transfers between devices  9.53 us (14%)
  local copies, waits for them, and re-layouts  3.37 us (5%)
    ppermute x12, starting transfers between devices, send(): moved.append(lax.ppermute(parts[shift], 'mem', ways))  23 us
    pallas_call x2, Pallas kernels, analyse(): pl.pallas_call(functools.partial(analyse_kernel, chunk, n_mem), in_specs=...  10.5 us
    ppermute x12, waiting for transfers between devices, send(): moved.append(lax.ppermute(parts[shift], 'mem', ways))  9.52 us
    pallas_call x2, Pallas kernels, forecast(): pl.pallas_call(functools.partial(forecast_kernel, chunk, n_mem), in_specs...  9.08 us
    pallas_call x1, Pallas kernels, gather(): pl.pallas_call(functools.partial(gather_kernel, n_mem), grid=(local // bl...  3.62 us
    unnamed x32, local copies, waits for them, and re-layouts  3.37 us
    all_to_all x1, starting transfers between devices, shards(): lax.all_to_all(counts, 'slab', split_axis=0, concat_axis=0, tiled=True)  3.35 us
    ppermute x1, starting transfers between devices, shards(): below = lax.ppermute(head, 'slab', down)  2.93 us
  transfers between devices with their start and end apart: 15, of which 2 were waited for; matrix products, arithmetic and copies ran while one was open for 1% of the time, Pallas kernels for 25%

profile of v2, /device:TPU:0, one launch (start us, length us, event | category | flops | bytes accessed | tf_op | source)
XLA Modules:
  0.0 68.9 jit_solution(10946552273042267593)
XLA Ops:
  0.0 4.5 %forecast0.1 = (f32[4,72,128]{2,1,0:T(8,128)}, f32[4,72,128]{2,1,0:T(8,128)}, f32[4,64,128]{2,1,0:T(8,128)}, f32[4,64,128]{2,1,0:T(8,128)}, f32[4,64,128]{2,1,0:T(8,128)}, /*index=5*/f32[4,64,128]{2,1,0:T(8,128)}) custom-call(s32[1]{0:T(128)} %bitcast.refs_0_.place, f32[2048,128]{1,0:T(8,128)} %bitcast.7, f32[32,128]{1,0:T(8,128)} %refs_2_.3, ...), custom_call_target="tpu_custom_call" | custom-call | tf_op jit(solution)/shard_map/forecast0/pallas_call | solution.py:89
  4.5 0.0 copy-start.15
  4.5 0.5 collective-permute-start.6
  5.0 2.9 %collective-permute-start.7 = (f32[4,72,128]{2,1,0:T(8,128)}, f32[4,72,128]{2,1,0:T(8,128)S(1)}, u32[]{:S(2)}, u32[]{:S(2)}) collective-permute-start(f32[4,72,128]{2,1,0:T(8,128)} %get-tuple-element.32), channel_id=1, source_target_pairs={{1,0},{2,1},{3,2},{4,3},{5,4},{6,5},{7,6},{0,7},{9,8},{10,9},{11,1... | collective-permute-start | bytes 442376 | tf_op jit(solution)/shard_map/ppermute | solution.py:293
  8.0 2.3 %collective-permute-start = (f32[4,64,128]{2,1,0:T(8,128)}, f32[4,64,128]{2,1,0:T(8,128)S(1)}, u32[]{:S(2)}, u32[]{:S(2)}) collective-permute-start(f32[4,64,128]{2,1,0:T(8,128)} %get-tuple-element.24), channel_id=1, source_target_pairs={{0,8},{8,16},{16,24},{24,0},{1,9},{9,17},{17,25},{25,1},{2,10},{10... | collective-permute-start | bytes 393224 | tf_op jit(solution)/shard_map/ppermute | solution.py:288
  10.2 2.6 %collective-permute-start.1 = (f32[4,64,128]{2,1,0:T(8,128)}, f32[4,64,128]{2,1,0:T(8,128)S(1)}, u32[]{:S(2)}, u32[]{:S(2)}) collective-permute-start(f32[4,64,128]{2,1,0:T(8,128)} %get-tuple-element.25), channel_id=1, source_target_pairs={{0,16},{8,24},{16,0},{24,8},{1,17},{9,25},{17,1},{25,9},{2,18},{10... | collective-permute-start | bytes 393224 | tf_op jit(solution)/shard_map/ppermute | solution.py:288
  12.8 1.3 %collective-permute-start.2 = (f32[4,64,128]{2,1,0:T(8,128)}, f32[4,64,128]{2,1,0:T(8,128)S(1)}, u32[]{:S(2)}, u32[]{:S(2)}) collective-permute-start(f32[4,64,128]{2,1,0:T(8,128)} %get-tuple-element.26), channel_id=1, source_target_pairs={{0,24},{8,0},{16,8},{24,16},{1,25},{9,1},{17,9},{25,17},{2,26},{10... | collective-permute-start | bytes 393224 | tf_op jit(solution)/shard_map/ppermute | solution.py:288
  14.2 0.0 copy-done.15
  14.2 0.6 reduce
  14.8 2.2 %tally.1 = f32[8,2,8,128]{3,2,1,0:T(8,128)} custom-call(f32[10,128]{1,0:T(8,128)} %bitcast.10, f32[10,128]{1,0:T(8,128)} %bitcast.11, s32[10,128]{1,0:T(8,128)} %bitcast.9, s32[10,128]{1,0:T(8,128)} %bitcast.12), custom_call_target="tpu_custom_call" | custom-call | tf_op jit(solution)/shard_map/tally/pallas_call | solution.py:135
  17.0 3.3 %all-to-all-start = ((f32[8,2,8,128]{3,2,1,0:T(8,128)}), f32[8,2,8,128]{3,2,1,0:T(8,128)S(1)}, u32[]{:S(2)}, u32[]{:S(2)}) async-start(f32[8,2,8,128]{3,2,1,0:T(8,128)} %tally.1), calls=%async_computation | async-start | bytes 131072 | tf_op jit(solution)/shard_map/all_to_all | solution.py:296
  20.3 0.0 collective-permute-done.6.refs_4_
  20.4 0.0 copy-start.1
  20.4 0.0 collective-permute-done.7.refs_5_
  20.4 0.6 copy-done.1
  21.0 0.0 copy-start.2
  21.0 0.7 copy-done.2
  21.7 4.6 %forecast1.1 = (f32[4,64,128]{2,1,0:T(8,128)}, f32[4,64,128]{2,1,0:T(8,128)}, f32[4,64,128]{2,1,0:T(8,128)}, f32[4,64,128]{2,1,0:T(8,128)}) custom-call(s32[1]{0:T(128)} %bitcast.refs_0_.place, f32[2048,128]{1,0:T(8,128)} %bitcast.8, f32[32,128]{1,0:T(8,128)} %refs_2_.3, f32[2,32,128]{2,1,0:T(8,128)} %refs_3_.3, f32[4,72,128]{2,1,0:T(8,128)} %copy-done.1, ...), custom_call_target="tpu_custom_call" | custom-call | tf_op jit(solution)/shard_map/forecast1/pallas_call | solution.py:89
  26.2 0.7 collective-permute-start.8
  26.9 0.3 collective-permute-start.9
  27.2 0.0 collective-permute-done.refs_1_
  27.3 2.9 %collective-permute-start.10 = (f32[4,64,128]{2,1,0:T(8,128)}, f32[4,64,128]{2,1,0:T(8,128)S(1)}, u32[]{:S(2)}, u32[]{:S(2)}) collective-permute-start(f32[4,64,128]{2,1,0:T(8,128)} %get-tuple-element.36), channel_id=1, source_target_pairs={{0,24},{8,0},{16,8},{24,16},{1,25},{9,1},{17,9},{25,17},{2,26},{10... | collective-permute-start | bytes 393224 | tf_op jit(solution)/shard_map/ppermute | solution.py:288
  30.1 0.0 all-to-all-done.tallies_ref
  30.1 0.0 copy-start
  30.1 0.0 collective-permute-done.1.refs_2_
  30.1 0.0 copy-start.11
  30.1 0.0 collective-permute-done.2.refs_3_
  30.2 0.0 copy-start.13
  30.2 0.0 copy-done.9
  30.2 0.6 copy-done
  30.7 0.0 copy-done.11
  30.8 0.1 copy-done.13
  30.9 5.2 %analyse0.1 = (f32[4,64,128]{2,1,0:T(8,128)}, f32[4,64,128]{2,1,0:T(8,128)}, f32[4,64,128]{2,1,0:T(8,128)}, f32[4,64,128]{2,1,0:T(8,128)}) custom-call(s32[1]{0:T(128)} %bitcast.refs_0_.place, f32[8,2,8,128]{3,2,1,0:T(8,128)} %copy-done, f32[4,64,128]{2,1,0:T(8,128)} %get-tuple-element.23.refs_0_, f32[4,64,128]{2,1,0:T(8,128)} %copy-done.9, ...), custom_call_target="tpu_custom_call" | custom-call | tf_op jit(solution)/shard_map/analyse0/pallas_call | solution.py:236
  36.1 1.2 %collective-permute-start.3 = (f32[4,64,128]{2,1,0:T(8,128)}, f32[4,64,128]{2,1,0:T(8,128)S(1)}, u32[]{:S(2)}, u32[]{:S(2)}) collective-permute-start(f32[4,64,128]{2,1,0:T(8,128)} %get-tuple-element.28), channel_id=1, source_target_pairs={{0,24},{8,0},{16,8},{24,16},{1,25},{9,1},{17,9},{25,17},{2,26},{10... | collective-permute-start | bytes 393224 | tf_op jit(solution)/shard_map/ppermute | solution.py:288
  37.3 0.8 %collective-permute-start.4 = (f32[4,64,128]{2,1,0:T(8,128)}, f32[4,64,128]{2,1,0:T(8,128)S(1)}, u32[]{:S(2)}, u32[]{:S(2)}) collective-permute-start(f32[4,64,128]{2,1,0:T(8,128)} %get-tuple-element.29), channel_id=1, source_target_pairs={{0,16},{8,24},{16,0},{24,8},{1,17},{9,25},{17,1},{25,9},{2,18},{10... | collective-permute-start | bytes 393224 | tf_op jit(solution)/shard_map/ppermute | solution.py:288
  38.1 0.0 collective-permute-done.8.refs_1_
  38.1 0.0 copy-start.10
  38.1 2.0 %collective-permute-start.5 = (f32[4,64,128]{2,1,0:T(8,128)}, f32[4,64,128]{2,1,0:T(8,128)S(1)}, u32[]{:S(2)}, u32[]{:S(2)}) collective-permute-start(f32[4,64,128]{2,1,0:T(8,128)} %get-tuple-element.30), channel_id=1, source_target_pairs={{0,8},{8,16},{16,24},{24,0},{1,9},{9,17},{17,25},{25,1},{2,10},{10... | collective-permute-start | bytes 393224 | tf_op jit(solution)/shard_map/ppermute | solution.py:288
  40.1 0.0 collective-permute-done.9.refs_2_
  40.1 0.0 copy-start.12
  40.1 0.0 collective-permute-done.10.refs_3_
  40.1 0.0 copy-start.14
  40.1 0.0 copy-done.10
  40.1 0.6 copy-done.12
  40.7 0.1 copy-done.14
  40.8 5.2 %analyse1.1 = (f32[4,64,128]{2,1,0:T(8,128)}, f32[4,64,128]{2,1,0:T(8,128)}, f32[4,64,128]{2,1,0:T(8,128)}, f32[4,64,128]{2,1,0:T(8,128)}) custom-call(s32[1]{0:T(128)} %bitcast.refs_0_.place, f32[8,2,8,128]{3,2,1,0:T(8,128)} %copy-done, f32[4,64,128]{2,1,0:T(8,128)} %get-tuple-element.33.refs_0_, f32[4,64,128]{2,1,0:T(8,128)} %copy-done.10, ...), custom_call_target="tpu_custom_call" | custom-call | tf_op jit(solution)/shard_map/analyse1/pallas_call | solution.py:236
  46.1 8.4 %collective-permute-start.11 = (f32[4,64,128]{2,1,0:T(8,128)}, f32[4,64,128]{2,1,0:T(8,128)S(1)}, u32[]{:S(2)}, u32[]{:S(2)}) collective-permute-start(f32[4,64,128]{2,1,0:T(8,128)} %get-tuple-element.38), channel_id=1, source_target_pairs={{0,24},{8,0},{16,8},{24,16},{1,25},{9,1},{17,9},{25,17},{2,26},{10... | collective-permute-start | bytes 393224 | tf_op jit(solution)/shard_map/ppermute | solution.py:288
  54.4 0.0 collective-permute-start.12
  54.4 0.0 collective-permute-done.3.refs_1_
  54.4 0.0 copy-start.3
  54.5 0.6 collective-permute-start.13
  55.0 0.0 collective-permute-done.4.refs_2_
  55.0 0.0 collective-permute-done.5.refs_3_
  55.0 0.0 copy-start.5
  55.0 3.4 %collective-permute-done.11.refs_5_ = f32[4,64,128]{2,1,0:T(8,128)S(1)} collective-permute-done((f32[4,64,128]{2,1,0:T(8,128)}, f32[4,64,128]{2,1,0:T(8,128)S(1)}, u32[]{:S(2)}, u32[]{:S(2)}) %collective-permute-start.11) | collective-permute-done | bytes 131104 | tf_op jit(solution)/shard_map/ppermute | solution.py:288
  58.4 6.1 %collective-permute-done.12.refs_6_ = f32[4,64,128]{2,1,0:T(8,128)S(1)} collective-permute-done((f32[4,64,128]{2,1,0:T(8,128)}, f32[4,64,128]{2,1,0:T(8,128)S(1)}, u32[]{:S(2)}, u32[]{:S(2)}) %collective-permute-start.12) | collective-permute-done | bytes 131104 | tf_op jit(solution)/shard_map/ppermute | solution.py:288
  64.5 0.0 collective-permute-done.13.refs_7_
  64.5 0.0 copy-done.3
  64.5 0.0 copy-done.4
  64.6 0.0 copy-done.5
  64.6 0.0 copy-done.6
  64.6 0.6 copy-done.7
  65.2 0.1 copy-done.8
  65.2 3.6 %gather.1 = f32[2048,128]{1,0:T(8,128)} custom-call(s32[1]{0:T(128)} %bitcast.refs_0_.place, f32[4,64,128]{2,1,0:T(8,128)} %get-tuple-element.27.refs_0_, f32[4,64,128]{2,1,0:T(8,128)} %copy-done.3, f32[4,64,128]{2,1,0:T(8,128)} %copy-done.4, f32[4,64,128]{2,1,0:T(8,128)} %copy-done.5, f32[4,64,128]{2,1,0:T(8,128)} %get-tuple-element.37.refs_4_, ...), custom_call_target="tpu_custom_call" | custom-call | tf_op jit(solution)/shard_map/gather/pallas_call | solution.py:265
  (5 shorter events, 0.0 us)
Async XLA Ops:
  4.5 9.7 %copy-start.15 = (s32[1280,1]{0,1:T(1,128)S(1)}, s32[1280,1]{0,1:T(1,128)}, u32[]{:S(2)}) copy-start(s32[1280,1]{0,1:T(1,128)} %param.12) | copy-start | bytes 15364
  4.5 15.8 %collective-permute-start.6 = (f32[4,72,128]{2,1,0:T(8,128)}, f32[4,72,128]{2,1,0:T(8,128)S(1)}, u32[]{:S(2)}, u32[]{:S(2)}) collective-permute-start(f32[4,72,128]{2,1,0:T(8,128)} %get-tuple-element.31), channel_id=1, source_target_pairs={{0,1},{1,2},{2,3},{3,4},{4,5},{5,6},{6,7},{7,0},{8,9},{9,10},{10,1... | collective-permute-start | bytes 442376 | tf_op jit(solution)/shard_map/ppermute | solution.py:292
  5.0 15.3 %collective-permute-start.7 = (f32[4,72,128]{2,1,0:T(8,128)}, f32[4,72,128]{2,1,0:T(8,128)S(1)}, u32[]{:S(2)}, u32[]{:S(2)}) collective-permute-start(f32[4,72,128]{2,1,0:T(8,128)} %get-tuple-element.32), channel_id=1, source_target_pairs={{1,0},{2,1},{3,2},{4,3},{5,4},{6,5},{7,6},{0,7},{9,8},{10,9},{11,1... | collective-permute-start | bytes 442376 | tf_op jit(solution)/shard_map/ppermute | solution.py:293
  8.0 19.3 %collective-permute-start = (f32[4,64,128]{2,1,0:T(8,128)}, f32[4,64,128]{2,1,0:T(8,128)S(1)}, u32[]{:S(2)}, u32[]{:S(2)}) collective-permute-start(f32[4,64,128]{2,1,0:T(8,128)} %get-tuple-element.24), channel_id=1, source_target_pairs={{0,8},{8,16},{16,24},{24,0},{1,9},{9,17},{17,25},{25,1},{2,10},{10... | collective-permute-start | bytes 393224 | tf_op jit(solution)/shard_map/ppermute | solution.py:288
  10.2 19.9 %collective-permute-start.1 = (f32[4,64,128]{2,1,0:T(8,128)}, f32[4,64,128]{2,1,0:T(8,128)S(1)}, u32[]{:S(2)}, u32[]{:S(2)}) collective-permute-start(f32[4,64,128]{2,1,0:T(8,128)} %get-tuple-element.25), channel_id=1, source_target_pairs={{0,16},{8,24},{16,0},{24,8},{1,17},{9,25},{17,1},{25,9},{2,18},{10... | collective-permute-start | bytes 393224 | tf_op jit(solution)/shard_map/ppermute | solution.py:288
  12.8 17.3 %collective-permute-start.2 = (f32[4,64,128]{2,1,0:T(8,128)}, f32[4,64,128]{2,1,0:T(8,128)S(1)}, u32[]{:S(2)}, u32[]{:S(2)}) collective-permute-start(f32[4,64,128]{2,1,0:T(8,128)} %get-tuple-element.26), channel_id=1, source_target_pairs={{0,24},{8,0},{16,8},{24,16},{1,25},{9,1},{17,9},{25,17},{2,26},{10... | collective-permute-start | bytes 393224 | tf_op jit(solution)/shard_map/ppermute | solution.py:288
  17.0 13.1 %all-to-all-start = ((f32[8,2,8,128]{3,2,1,0:T(8,128)}), f32[8,2,8,128]{3,2,1,0:T(8,128)S(1)}, u32[]{:S(2)}, u32[]{:S(2)}) async-start(f32[8,2,8,128]{3,2,1,0:T(8,128)} %tally.1), calls=%async_computation | async-start | bytes 131072 | tf_op jit(solution)/shard_map/all_to_all | solution.py:296
  20.4 0.7 copy-start.1
  21.0 0.7 copy-start.2
  26.2 11.9 %collective-permute-start.8 = (f32[4,64,128]{2,1,0:T(8,128)}, f32[4,64,128]{2,1,0:T(8,128)S(1)}, u32[]{:S(2)}, u32[]{:S(2)}) collective-permute-start(f32[4,64,128]{2,1,0:T(8,128)} %get-tuple-element.34), channel_id=1, source_target_pairs={{0,8},{8,16},{16,24},{24,0},{1,9},{9,17},{17,25},{25,1},{2,10},{10... | collective-permute-start | bytes 393224 | tf_op jit(solution)/shard_map/ppermute | solution.py:288
  26.9 13.2 %collective-permute-start.9 = (f32[4,64,128]{2,1,0:T(8,128)}, f32[4,64,128]{2,1,0:T(8,128)S(1)}, u32[]{:S(2)}, u32[]{:S(2)}) collective-permute-start(f32[4,64,128]{2,1,0:T(8,128)} %get-tuple-element.35), channel_id=1, source_target_pairs={{0,16},{8,24},{16,0},{24,8},{1,17},{9,25},{17,1},{25,9},{2,18},{10... | collective-permute-start | bytes 393224 | tf_op jit(solution)/shard_map/ppermute | solution.py:288
  27.2 2.9 %copy-start.9 = (f32[4,64,128]{2,1,0:T(8,128)}, f32[4,64,128]{2,1,0:T(8,128)S(1)}, u32[]{:S(2)}) copy-start(f32[4,64,128]{2,1,0:T(8,128)S(1)} %collective-permute-done.refs_1_) | copy-start | bytes 393220
  27.3 12.8 %collective-permute-start.10 = (f32[4,64,128]{2,1,0:T(8,128)}, f32[4,64,128]{2,1,0:T(8,128)S(1)}, u32[]{:S(2)}, u32[]{:S(2)}) collective-permute-start(f32[4,64,128]{2,1,0:T(8,128)} %get-tuple-element.36), channel_id=1, source_target_pairs={{0,24},{8,0},{16,8},{24,16},{1,25},{9,1},{17,9},{25,17},{2,26},{10... | collective-permute-start | bytes 393224 | tf_op jit(solution)/shard_map/ppermute | solution.py:288
  30.1 0.6 copy-start
  30.1 0.7 copy-start.11
  30.2 0.7 %copy-start.13 = (f32[4,64,128]{2,1,0:T(8,128)}, f32[4,64,128]{2,1,0:T(8,128)S(1)}, u32[]{:S(2)}) copy-start(f32[4,64,128]{2,1,0:T(8,128)S(1)} %collective-permute-done.2.refs_3_) | copy-start | bytes 393220
  36.1 18.3 %collective-permute-start.3 = (f32[4,64,128]{2,1,0:T(8,128)}, f32[4,64,128]{2,1,0:T(8,128)S(1)}, u32[]{:S(2)}, u32[]{:S(2)}) collective-permute-start(f32[4,64,128]{2,1,0:T(8,128)} %get-tuple-element.28), channel_id=1, source_target_pairs={{0,24},{8,0},{16,8},{24,16},{1,25},{9,1},{17,9},{25,17},{2,26},{10... | collective-permute-start | bytes 393224 | tf_op jit(solution)/shard_map/ppermute | solution.py:288
  37.3 17.7 %collective-permute-start.4 = (f32[4,64,128]{2,1,0:T(8,128)}, f32[4,64,128]{2,1,0:T(8,128)S(1)}, u32[]{:S(2)}, u32[]{:S(2)}) collective-permute-start(f32[4,64,128]{2,1,0:T(8,128)} %get-tuple-element.29), channel_id=1, source_target_pairs={{0,16},{8,24},{16,0},{24,8},{1,17},{9,25},{17,1},{25,9},{2,18},{10... | collective-permute-start | bytes 393224 | tf_op jit(solution)/shard_map/ppermute | solution.py:288
  38.1 2.0 %copy-start.10 = (f32[4,64,128]{2,1,0:T(8,128)}, f32[4,64,128]{2,1,0:T(8,128)S(1)}, u32[]{:S(2)}) copy-start(f32[4,64,128]{2,1,0:T(8,128)S(1)} %collective-permute-done.8.refs_1_) | copy-start | bytes 393220
  38.1 16.9 %collective-permute-start.5 = (f32[4,64,128]{2,1,0:T(8,128)}, f32[4,64,128]{2,1,0:T(8,128)S(1)}, u32[]{:S(2)}, u32[]{:S(2)}) collective-permute-start(f32[4,64,128]{2,1,0:T(8,128)} %get-tuple-element.30), channel_id=1, source_target_pairs={{0,8},{8,16},{16,24},{24,0},{1,9},{9,17},{17,25},{25,1},{2,10},{10... | collective-permute-start | bytes 393224 | tf_op jit(solution)/shard_map/ppermute | solution.py:288
  40.1 0.6 copy-start.12
  40.1 0.7 %copy-start.14 = (f32[4,64,128]{2,1,0:T(8,128)}, f32[4,64,128]{2,1,0:T(8,128)S(1)}, u32[]{:S(2)}) copy-start(f32[4,64,128]{2,1,0:T(8,128)S(1)} %collective-permute-done.10.refs_3_) | copy-start | bytes 393220
  46.1 12.3 %collective-permute-start.11 = (f32[4,64,128]{2,1,0:T(8,128)}, f32[4,64,128]{2,1,0:T(8,128)S(1)}, u32[]{:S(2)}, u32[]{:S(2)}) collective-permute-start(f32[4,64,128]{2,1,0:T(8,128)} %get-tuple-element.38), channel_id=1, source_target_pairs={{0,24},{8,0},{16,8},{24,16},{1,25},{9,1},{17,9},{25,17},{2,26},{10... | collective-permute-start | bytes 393224 | tf_op jit(solution)/shard_map/ppermute | solution.py:288
  54.4 10.1 %collective-permute-start.12 = (f32[4,64,128]{2,1,0:T(8,128)}, f32[4,64,128]{2,1,0:T(8,128)S(1)}, u32[]{:S(2)}, u32[]{:S(2)}) collective-permute-start(f32[4,64,128]{2,1,0:T(8,128)} %get-tuple-element.39), channel_id=1, source_target_pairs={{0,16},{8,24},{16,0},{24,8},{1,17},{9,25},{17,1},{25,9},{2,18},{10... | collective-permute-start | bytes 393224 | tf_op jit(solution)/shard_map/ppermute | solution.py:288
  54.4 10.1 %copy-start.3 = (f32[4,64,128]{2,1,0:T(8,128)}, f32[4,64,128]{2,1,0:T(8,128)S(1)}, u32[]{:S(2)}) copy-start(f32[4,64,128]{2,1,0:T(8,128)S(1)} %collective-permute-done.3.refs_1_) | copy-start | bytes 393220
  54.5 10.1 %collective-permute-start.13 = (f32[4,64,128]{2,1,0:T(8,128)}, f32[4,64,128]{2,1,0:T(8,128)S(1)}, u32[]{:S(2)}, u32[]{:S(2)}) collective-permute-start(f32[4,64,128]{2,1,0:T(8,128)} %get-tuple-element.40), channel_id=1, source_target_pairs={{0,8},{8,16},{16,24},{24,0},{1,9},{9,17},{17,25},{25,1},{2,10},{10... | collective-permute-start | bytes 393224 | tf_op jit(solution)/shard_map/ppermute | solution.py:288
  55.0 9.5 %copy-start.4 = (f32[4,64,128]{2,1,0:T(8,128)}, f32[4,64,128]{2,1,0:T(8,128)S(1)}, u32[]{:S(2)}) copy-start(f32[4,64,128]{2,1,0:T(8,128)S(1)} %collective-permute-done.4.refs_2_) | copy-start | bytes 393220
  55.0 9.5 %copy-start.5 = (f32[4,64,128]{2,1,0:T(8,128)}, f32[4,64,128]{2,1,0:T(8,128)S(1)}, u32[]{:S(2)}) copy-start(f32[4,64,128]{2,1,0:T(8,128)S(1)} %collective-permute-done.5.refs_3_) | copy-start | bytes 393220
  58.4 6.2 %copy-start.6 = (f32[4,64,128]{2,1,0:T(8,128)}, f32[4,64,128]{2,1,0:T(8,128)S(1)}, u32[]{:S(2)}) copy-start(f32[4,64,128]{2,1,0:T(8,128)S(1)} %collective-permute-done.11.refs_5_) | copy-start | bytes 393220
  64.5 0.7 copy-start.7
  64.5 0.7 %copy-start.8 = (f32[4,64,128]{2,1,0:T(8,128)}, f32[4,64,128]{2,1,0:T(8,128)S(1)}, u32[]{:S(2)}) copy-start(f32[4,64,128]{2,1,0:T(8,128)S(1)} %collective-permute-done.13.refs_7_) | copy-start | bytes 393220

commit v3 on v2

v3 whole, which is shorter than its diff:
```python
import functools

import jax
import jax.numpy as jnp
from jax import lax
from jax.experimental import pallas as pl
from jax.experimental.pallas import tpu as pltpu
from jax.sharding import PartitionSpec as P

STEPS = 4
NS_STEPS = 5
HALF = 4
SUB = 8
F32 = jnp.float32
BF16 = jnp.bfloat16

VMEM = pl.BlockSpec(memory_space=pltpu.VMEM)
SMEM = pl.BlockSpec(memory_space=pltpu.SMEM)
HBM = pl.BlockSpec(memory_space=pl.ANY)
PARAMS = pltpu.CompilerParams(vmem_limit_bytes=16 << 20)


def near(arrays):
    return [pltpu.with_memory_space_constraint(a, pltpu.VMEM) for a in arrays]


def put_table(table, row, diffuse, drift_x, drift_y):
    width = diffuse.shape[-1]
    parts = (
        1.0 - 4.0 * diffuse,
        diffuse - 0.5 * drift_x,
        diffuse + 0.5 * drift_x,
        diffuse + 0.5 * drift_y,
        diffuse - 0.5 * drift_y,
    )
    for k, part in enumerate(parts):
        for r in range(part.shape[0]):
            table[row + r, k] = jnp.broadcast_to(part[r : r + 1], (SUB, width))


def advance(field, scratch, table, first, count):
    members, width = field.shape[1:]
    source = field
    for step in range(STEPS):
        target = scratch[step % 2]
        for i in range(first + step + 1, first + count - step - 1):
            coef = [table[i, k] for k in range(5)]
            for m in range(0, members, SUB):
                at = pl.ds(m, SUB)
                center = source[i, at, :]
                target[i, at, :] = (
                    (center * coef[0] + pltpu.roll(center, width - 1, 1) * coef[1])
                    + (pltpu.roll(center, 1, 1) * coef[2] + source[i - 1, at, :] * coef[3])
                    + source[i + 1, at, :] * coef[4]
                )
        source = target
    return source


def inner_kernel(n_mem, *refs):
    place, ens_ref, diffuse_ref, drift_ref = refs[:4]
    edges, early, late = refs[4:6], refs[6 : 6 + n_mem], refs[6 + n_mem : 6 + 2 * n_mem]
    field, table, ping, pong = refs[6 + 2 * n_mem :]
    rows, width = diffuse_ref.shape
    members = ens_ref.shape[0] // rows

    for r in range(rows):
        field[r] = ens_ref[pl.ds(r, members, stride=rows), :]
    put_table(table, 0, diffuse_ref[...], drift_ref[0], drift_ref[1])
    for edge, first in zip(edges, (0, rows - STEPS)):
        for r in range(STEPS):
            row = first + r
            edge[r, :members, :] = field[row]
            edge[r, members : members + 1, :] = diffuse_ref[row : row + 1, :]
            for k in range(2):
                edge[r, members + 1 + k : members + 2 + k, :] = drift_ref[k, row : row + 1, :]

    done = advance(field, (ping, pong), table, 0, rows)
    for shift in range(n_mem):
        group = lax.rem(place[0] + shift, n_mem)
        top = group * SUB + jnp.where(group == 0, HALF, 0)
        bottom = jnp.minimum(group * SUB + HALF, rows - 2 * HALF)
        for r in range(HALF):
            early[shift][r] = done[top + r]
            late[shift][r] = done[bottom + r]


def inner(n_mem, place, ens, diffusivity, velocity):
    rows, width = diffusivity.shape
    members = ens.shape[0] // rows
    part = pltpu.VMEM((HALF, members, width), F32)
    edge = pltpu.VMEM((STEPS, members + SUB, width), F32)
    shapes = [edge] * 2 + [part] * (2 * n_mem)
    outs = pl.pallas_call(
        functools.partial(inner_kernel, n_mem),
        in_specs=[SMEM] + [VMEM] * 3,
        out_specs=[VMEM] * len(shapes),
        out_shape=shapes,
        scratch_shapes=[
            pltpu.VMEM((rows, members, width), F32),
            pltpu.VMEM((rows, 5, SUB, width), F32),
            pltpu.VMEM((rows, members, width), F32),
            pltpu.VMEM((rows, members, width), F32),
        ],
        compiler_params=PARAMS,
        name="inner",
    )(place, ens, diffusivity, velocity)
    return outs[:2], outs[2 : 2 + n_mem], outs[2 + n_mem :]


def outer_kernel(n_mem, *refs):
    place, top_ref, bottom_ref, diffuse_ref, drift_ref, above, below = refs[:7]
    outs = refs[7 + n_mem : 7 + 2 * n_mem]
    field, table, ping, pong = refs[7 + 2 * n_mem :]
    rows = diffuse_ref.shape[0]
    members = field.shape[1]
    span = 3 * STEPS
    lows = (0, rows - 2 * STEPS)

    for side, ref in enumerate((top_ref, bottom_ref)):
        halo = (above, below)[side]
        inside = side * span + (1 - side) * STEPS
        outside = side * span + side * 2 * STEPS
        part = ref.reshape(members * SUB, ref.shape[-1])
        for r in range(SUB):
            field[inside + r] = part[pl.ds(r, members, stride=SUB), :]
        rows_at = pl.ds(lows[side], SUB)
        put_table(table, inside, diffuse_ref[rows_at], drift_ref[0, rows_at], drift_ref[1, rows_at])
        for r in range(STEPS):
            field[outside + r] = halo[r, :members, :]
            put_table(
                table, outside + r, *(halo[r, members + k : members + k + 1, :] for k in range(3))
            )
        done = advance(field, (ping, pong), table, side * span, span)

    for shift in range(n_mem):
        group = lax.rem(place[0] + shift, n_mem)

        @pl.when((group == 0) | (group == n_mem - 1))
        def _(group=group, shift=shift):
            start = jnp.where(group == 0, 0, span) + STEPS
            for r in range(HALF):
                outs[shift][r] = done[start + r]


def outer(n_mem, place, ens, diffusivity, velocity, halos, late):
    rows, width = diffusivity.shape
    members = ens.shape[0]
    span = 6 * STEPS
    late = near(late)
    block = (members, SUB, width)
    whole = [pl.BlockSpec(a.shape, lambda i, n=a.ndim: (0,) * n) for a in (diffusivity, velocity)]
    return pl.pallas_call(
        functools.partial(outer_kernel, n_mem),
        grid=(1,),
        in_specs=[
            SMEM,
            pl.BlockSpec(block, lambda i: (0, 0, 0)),
            pl.BlockSpec(block, lambda i: (0, rows // SUB - 1, 0)),
        ]
        + whole
        + [VMEM] * (2 + n_mem),
        out_specs=[VMEM] * n_mem,
        out_shape=[pltpu.VMEM(a.shape, F32) for a in late],
        scratch_shapes=[
            pltpu.VMEM((span, members, width), F32),
            pltpu.VMEM((span, 5, SUB, width), F32),
            pltpu.VMEM((span, members, width), F32),
            pltpu.VMEM((span, members, width), F32),
        ],
        input_output_aliases={7 + k: k for k in range(n_mem)},
        compiler_params=PARAMS,
        name="outer",
    )(place, ens, ens, diffusivity, velocity, *near(halos), *late)


def tally_kernel(value_ref, weight_ref, slab_ref, cell_ref, out_ref):
    lanes = out_ref.shape[-1]
    blocks = value_ref.shape[1] // lanes
    n_slab = out_ref.shape[0]
    width = out_ref.shape[-1]
    bins = n_slab * SUB
    bin_id = lax.broadcasted_iota(jnp.int32, (bins, lanes), 0)
    column_id = lax.broadcasted_iota(jnp.int32, (width, lanes), 0)
    totals = jnp.zeros((2 * bins, width), F32)
    for b in range(blocks):
        at = pl.ds(b * lanes, lanes)
        cell = cell_ref[:, at]
        weight = weight_ref[:, at]
        product = weight * value_ref[:, at]
        named = slab_ref[:, at] * SUB + cell // width
        here = bin_id == named
        column = jnp.where(column_id == cell % width, 1.0, 0.0).astype(BF16)
        rest = jnp.concatenate(
            [jnp.where(here, weight, 0.0), jnp.where(here, product, 0.0)], axis=0
        )
        for _ in range(3):
            piece = rest.astype(BF16)
            rest = rest - piece.astype(F32)
            totals = totals + lax.dot_general(
                piece, column, (((1,), (1,)), ((), ())), preferred_element_type=F32
            )
    for k in range(2 * n_slab):
        out_ref[k % n_slab, k // n_slab] = totals[k * SUB : (k + 1) * SUB]


def tally(value, weight, slab, cell, n_slab, width):
    return pl.pallas_call(
        tally_kernel,
        in_specs=[VMEM] * 4,
        out_specs=VMEM,
        out_shape=pltpu.VMEM((n_slab, 2, SUB, width), F32),
        compiler_params=PARAMS,
        name="tally",
    )(*(a.reshape(1, -1) for a in (value, weight, slab, cell)))


def halves(a):
    high = a.astype(BF16)
    return high, (a - high.astype(F32)).astype(BF16)


def left(a):
    return jnp.concatenate(halves(a), axis=1)


def right(b):
    both = jnp.concatenate(halves(b), axis=1)
    return jnp.concatenate([both, both], axis=0)


def product(a, b):
    both = jnp.dot(a, b, preferred_element_type=F32)
    width = both.shape[1] // 2
    return both[:, :width] + both[:, width:]


def analyse_kernel(chunk, n_mem, place, tallies_ref, *refs):
    fields, outs, spread = refs[:n_mem], refs[n_mem : 2 * n_mem], refs[2 * n_mem]
    local, width = fields[0].shape[1:]
    members = n_mem * local
    n_slab = tallies_ref.shape[0]
    eye = lax.broadcasted_iota(jnp.int32, (width, width), 0) == lax.broadcasted_iota(
        jnp.int32, (width, width), 1
    )
    total = tallies_ref[0]
    for k in range(1, n_slab):
        total = total + tallies_ref[k]
    first_half = (place[0] == 0) if chunk else (place[0] != 0)
    total = jnp.where(first_half, total[:, :HALF], total[:, HALF:])
    patches = range(HALF)

    means, grams, iterates, scales, gaps = [], [], [], [], []
    for p in patches:
        weight = total[0, p : p + 1, :]
        mean = sum(jnp.sum(f[p], axis=0, keepdims=True) for f in fields) * (1.0 / members)
        for k, f in enumerate(fields):
            spread[p, k * local : (k + 1) * local, :] = (f[p] - mean).astype(BF16)
        s = spread[p]
        gram = lax.dot_general(s, s, (((0,), (0,)), ((), ())), preferred_element_type=F32)
        scaled = gram * weight
        trace = jnp.sum(jnp.where(eye, scaled, 0.0), keepdims=True)
        square = jnp.sum(scaled * scaled.T, keepdims=True)
        norm = (members - 1.0) ** 2 * members + 2.0 * (members - 1.0) * trace + square
        scale = 8.0 * jnp.sqrt(norm * (1.0 / members))
        inverse = 1.0 / scale
        iterates.append(scaled * inverse + jnp.where(eye, (members - 1.0) * inverse, 0.0))
        means.append(mean)
        grams.append(gram)
        scales.append(inverse)
        gaps.append(total[1, p : p + 1, :] - weight * mean)

    roots = [None] * HALF
    for step in range(NS_STEPS):
        last = step == NS_STEPS - 1
        if step == 0:
            both = iterates
        else:
            rights = [right(y) for y in iterates]
            both = [product(left(roots[p]), rights[p]) for p in patches]
        factors = [jnp.where(eye, 1.5, 0.0) - 0.5 * b for b in both]
        lefts = [left(f) for f in factors]
        if not last:
            iterates = [
                product(lefts[p], right(iterates[p]) if step == 0 else rights[p]) for p in patches
            ]
        if step == 0:
            roots = factors
        else:
            roots = [product(lefts[p], right(roots[p])) for p in patches]

    for p in patches:
        root = right(roots[p])
        line = jnp.broadcast_to(gaps[p], (SUB, width))
        line = product(left(line), root)
        line = product(left(line), root)
        line = product(left(line), right(grams[p]))
        base = means[p] + line[:1] * scales[p]
        transform = (jnp.sqrt((members - 1.0) * scales[p]) * roots[p]).astype(BF16)
        update = lax.dot_general(
            spread[p], transform, (((1,), (1,)), ((), ())), preferred_element_type=F32
        )
        for k, out in enumerate(outs):
            out[pl.ds(p, local, stride=HALF), :] = base + update[k * local : (k + 1) * local]


def analyse(chunk, n_mem, place, tallies, fields):
    local, width = fields[0].shape[1:]
    shape = pltpu.VMEM((local * HALF, width), F32)
    return pl.pallas_call(
        functools.partial(analyse_kernel, chunk, n_mem),
        in_specs=[SMEM] + [VMEM] * (1 + n_mem),
        out_specs=[VMEM] * n_mem,
        out_shape=[shape] * n_mem,
        scratch_shapes=[pltpu.VMEM((HALF, n_mem * local, width), BF16)],
        compiler_params=PARAMS,
        name=f"analyse{chunk}",
    )(place, *near([tallies, *fields]))


def settle_kernel(chunk, n_mem, place, *refs):
    parts, out_ref, sems = refs[:n_mem], refs[-2], refs[-1]
    copies = []
    for shift in range(n_mem):
        group = lax.rem(place[0] + shift, n_mem)
        second = (group != 0) if chunk else (group == 0)
        at = 2 * group + second.astype(jnp.int32)
        copies.append(pltpu.make_async_copy(parts[shift], out_ref.at[:, at], sems.at[shift]))
    for copy in copies:
        copy.start()
    for copy in copies:
        copy.wait()


def settle(chunk, n_mem, place, parts, out=None):
    local, width = parts[0].shape[0] // HALF, parts[0].shape[1]
    parts = near([a.reshape(local, HALF, width) for a in parts])
    return pl.pallas_call(
        functools.partial(settle_kernel, chunk, n_mem),
        in_specs=[SMEM] + [VMEM] * n_mem + [HBM] * chunk,
        out_specs=HBM,
        out_shape=jax.ShapeDtypeStruct((local, 2 * n_mem, HALF, width), F32),
        scratch_shapes=[pltpu.SemaphoreType.DMA((n_mem,))],
        input_output_aliases={1 + n_mem: 0} if chunk else {},
        compiler_params=PARAMS,
        name=f"settle{chunk}",
    )(place, *parts, *([out] if chunk else []))


def shards(ensemble, diffusivity, velocity, obs_value, obs_weight, obs_slab, obs_cell):
    n_slab, n_mem = lax.axis_size("slab"), lax.axis_size("mem")
    members, rows, width = ensemble.shape
    place = lax.axis_index("mem").reshape(1)
    assert rows == n_mem * SUB
    up = [(i, (i + 1) % n_slab) for i in range(n_slab)]
    down = [(j, i) for i, j in up]

    def send(parts, sign):
        moved = [parts[0]]
        for shift in range(1, n_mem):
            ways = [(i, (i + sign * shift) % n_mem) for i in range(n_mem)]
            moved.append(lax.ppermute(parts[shift], "mem", ways))
        return moved

    flat = ensemble.reshape(members * rows, width)
    (head, tail), early, late = inner(n_mem, place, flat, diffusivity, velocity)
    above = lax.ppermute(tail, "slab", up)
    below = lax.ppermute(head, "slab", down)
    early = send(early, 1)
    counts = tally(obs_value, obs_weight, obs_slab, obs_cell, n_slab, width)
    counts = lax.all_to_all(counts, "slab", split_axis=0, concat_axis=0, tiled=True)
    late = outer(n_mem, place, ensemble, diffusivity, velocity, (above, below), late)
    late = send(late, 1)
    early = send(analyse(0, n_mem, place, counts, early), -1)
    late = send(analyse(1, n_mem, place, counts, late), -1)
    out = settle(0, n_mem, place, early)
    return settle(1, n_mem, place, late, out).reshape(members, rows, width)


def solution(mesh):
    return jax.shard_map(
        shards,
        mesh=mesh,
        in_specs=(
            P("mem", "slab", None),
            P("slab", None),
            P(None, "slab", None),
            P(("mem", "slab")),
            P(("mem", "slab")),
            P(("mem", "slab"), None),
            P(("mem", "slab")),
        ),
        out_specs=P("mem", "slab", None),
        check_vma=False,
    )
```

time: 69.4 us -> 61.9 us (0.89)
  Pallas kernels: 25.4 us -> 13.3 us
  waiting for transfers between devices: 9.53 us -> 13.3 us
  local copies, waits for them, and re-layouts: 3.37 us -> 4.1 us
  starting transfers between devices: 29.8 us -> 30.5 us
    pallas_call x3 -> x4, Pallas kernels: 12.7 us -> 5.26 us  [the longest x1 2.53 us: inner(): pl.pallas_call(functools.partial(inner_kernel, n_mem), in_specs=[SMEM] +...]
    pallas_call x2, Pallas kernels: 10.5 us -> 6.63 us  [analyse(): pl.pallas_call(functools.partial(analyse_kernel, chunk, n_mem), in_specs=...]
    ppermute x12, waiting for transfers between devices: 9.52 us -> 13.3 us  [send(): moved.append(lax.ppermute(parts[shift], 'mem', ways))]
    pallas_call x1, Pallas kernels: 2.19 us -> 1.44 us  [tally(): pl.pallas_call(tally_kernel, in_specs=[VMEM] * 4, out_specs=VMEM, out_sha...]
    unnamed x32 -> x20, local copies, waits for them, and re-layouts: 3.37 us -> 4.08 us
  transfers between devices with their start and end apart: 15 -> 15, of which waited for: 2 -> 3; matrix products, arithmetic and copies ran while one was open for 1% -> 0% of each run, Pallas kernels for 25% -> 16%
where the time goes in v3:
time: 61.9 us; the launch traced here: 61.4 us
  starting transfers between devices  30.5 us (49%)
  Pallas kernels  13.3 us (21%)
  waiting for transfers between devices  13.3 us (21%)
  local copies, waits for them, and re-layouts  4.1 us (7%)
    ppermute x12, starting transfers between devices, send(): moved.append(lax.ppermute(parts[shift], 'mem', ways))  23.6 us
    ppermute x12, waiting for transfers between devices, send(): moved.append(lax.ppermute(parts[shift], 'mem', ways))  13.3 us
    pallas_call x2, Pallas kernels, analyse(): pl.pallas_call(functools.partial(analyse_kernel, chunk, n_mem), in_specs=...  6.63 us
    unnamed x20, local copies, waits for them, and re-layouts  4.08 us
    all_to_all x1, starting transfers between devices, shards(): lax.all_to_all(counts, 'slab', split_axis=0, concat_axis=0, tiled=True)  3.48 us
    ppermute x1, starting transfers between devices, shards(): below = lax.ppermute(head, 'slab', down)  2.93 us
    pallas_call x1, Pallas kernels, inner(): pl.pallas_call(functools.partial(inner_kernel, n_mem), in_specs=[SMEM] +...  2.53 us
    pallas_call x2, Pallas kernels, settle(): pl.pallas_call(functools.partial(settle_kernel, chunk, n_mem), in_specs=[...  1.64 us
  transfers between devices with their start and end apart: 15, of which 3 were waited for; matrix products, arithmetic and copies ran while one was open for 0% of the time, Pallas kernels for 16%

profile of v3, /device:TPU:0, one launch (start us, length us, event | category | flops | bytes accessed | tf_op | source)
XLA Modules:
  0.0 61.4 jit_solution(9393841143527084089)
XLA Ops:
  0.0 0.0 copy-start
  0.0 1.2 %copy-done = f32[64,32,128]{2,1,0:T(8,128)S(1)} copy-done((f32[64,32,128]{2,1,0:T(8,128)S(1)}, f32[64,32,128]{2,1,0:T(8,128)}, u32[]{:S(2)}) %copy-start) | copy-done | bytes 1048600
  1.2 0.0 copy-start.2
  1.2 0.8 %copy-done.2 = f32[2,32,128]{2,1,0:T(8,128)S(1)} copy-done((f32[2,32,128]{2,1,0:T(8,128)S(1)}, f32[2,32,128]{2,1,0:T(8,128)}, u32[]{:S(2)}) %copy-start.2) | copy-done | bytes 32792
  2.0 0.0 copy-start.4
  2.0 0.7 %copy-done.4 = f32[32,128]{1,0:T(8,128)S(1)} copy-done((f32[32,128]{1,0:T(8,128)S(1)}, f32[32,128]{1,0:T(8,128)}, u32[]{:S(2)}) %copy-start.4) | copy-done | bytes 16408
  2.7 0.0 copy-start.1
  2.7 2.5 %inner.1 = (f32[4,72,128]{2,1,0:T(8,128)S(1)}, f32[4,72,128]{2,1,0:T(8,128)S(1)}, f32[4,64,128]{2,1,0:T(8,128)S(1)}, f32[4,64,128]{2,1,0:T(8,128)S(1)}, f32[4,64...) custom-call(s32[1]{0:T(128)} %bitcast.refs_0_.place, ...), custom_call_target="tpu_custom_call" | custom-call | tf_op jit(solution)/shard_map/inner/pallas_call | solution.py:94
  5.2 0.0 copy-start.7
  5.3 0.5 collective-permute-start
  5.8 2.9 %collective-permute-start.1 = (f32[4,72,128]{2,1,0:T(8,128)S(1)}, f32[4,72,128]{2,1,0:T(8,128)S(1)}, u32[]{:S(2)}, u32[]{:S(2)}) collective-permute-start(f32[4,72,128]{2,1,0:T(8,128)S(1)} %get-tuple-element.28), channel_id=1, source_target_pairs={{1,0},{2,1},{3,2},{4,3},{5,4},{6,5},{7,6},{0,7},{9,8},{10,9},{11,1... | collective-permute-start | bytes 442376 | tf_op jit(solution)/shard_map/ppermute | solution.py:368
  8.7 0.0 copy-start.8
  8.7 2.3 %collective-permute-start.8 = (f32[4,64,128]{2,1,0:T(8,128)S(1)}, f32[4,64,128]{2,1,0:T(8,128)S(1)}, u32[]{:S(2)}, u32[]{:S(2)}) collective-permute-start(f32[4,64,128]{2,1,0:T(8,128)S(1)} %get-tuple-element.42), channel_id=1, source_target_pairs={{0,8},{8,16},{16,24},{24,0},{1,9},{9,17},{17,25},{25,1},{2,10},{10... | collective-permute-start | bytes 393224 | tf_op jit(solution)/shard_map/ppermute | solution.py:362
  11.0 2.6 %collective-permute-start.9 = (f32[4,64,128]{2,1,0:T(8,128)S(1)}, f32[4,64,128]{2,1,0:T(8,128)S(1)}, u32[]{:S(2)}, u32[]{:S(2)}) collective-permute-start(f32[4,64,128]{2,1,0:T(8,128)S(1)} %get-tuple-element.43), channel_id=1, source_target_pairs={{0,16},{8,24},{16,0},{24,8},{1,17},{9,25},{17,1},{25,9},{2,18},{10... | collective-permute-start | bytes 393224 | tf_op jit(solution)/shard_map/ppermute | solution.py:362
  13.6 1.3 %collective-permute-start.10 = (f32[4,64,128]{2,1,0:T(8,128)S(1)}, f32[4,64,128]{2,1,0:T(8,128)S(1)}, u32[]{:S(2)}, u32[]{:S(2)}) collective-permute-start(f32[4,64,128]{2,1,0:T(8,128)S(1)} %get-tuple-element.44), channel_id=1, source_target_pairs={{0,24},{8,0},{16,8},{24,16},{1,25},{9,1},{17,9},{25,17},{2,26},{10... | collective-permute-start | bytes 393224 | tf_op jit(solution)/shard_map/ppermute | solution.py:362
  14.9 0.0 copy-done.7
  15.0 0.0 copy-done.8
  15.0 0.0 copy-start.9
  15.0 0.7 %copy-done.9 = s32[1280]{0:T(1024)S(1)} copy-done((s32[1280]{0:T(1024)S(1)}, s32[1280]{0:T(1024)}, u32[]{:S(2)}) %copy-start.9) | copy-done | bytes 5144
  15.7 0.0 copy-start.6
  15.7 0.7 %copy-done.6 = s32[1280,1]{0,1:T(1,128)S(1)} copy-done((s32[1280,1]{0,1:T(1,128)S(1)}, s32[1280,1]{0,1:T(1,128)}, u32[]{:S(2)}) %copy-start.6) | copy-done | bytes 5144
  16.3 1.4 %tally.1 = f32[8,2,8,128]{3,2,1,0:T(8,128)} custom-call(f32[1,1280]{1,0:T(1,128)S(1)} %reshape.46.value_ref, f32[1,1280]{1,0:T(1,128)S(1)} %reshape.47.weight_ref, s32[1,1280]{1,0:T(1,128)S(1)} %bitcast.21, s32[1,1280]{1,0:T(1,128)S(1)} %reshape.49.cell_ref), custom_call_target="tpu_custom_call" | custom-call | tf_op jit(solution)/shard_map/tally/pallas_call | solution.py:208
  17.8 0.0 copy-start.3
  17.8 0.0 copy-start.5
  17.8 3.5 %all-to-all-start = ((f32[8,2,8,128]{3,2,1,0:T(8,128)}), f32[8,2,8,128]{3,2,1,0:T(8,128)S(1)}, u32[]{:S(2)}, u32[]{:S(2)}) async-start(f32[8,2,8,128]{3,2,1,0:T(8,128)} %tally.1), calls=%async_computation | async-start | bytes 131072 | tf_op jit(solution)/shard_map/all_to_all | solution.py:371
  21.3 0.0 collective-permute-done.refs_5_
  21.3 0.0 collective-permute-done.1.refs_6_
  21.3 0.0 copy-done.1
  21.3 0.0 copy-done.3
  21.3 0.0 copy-done.5
  21.3 1.1 %outer.1 = (f32[4,64,128]{2,1,0:T(8,128)S(1)}, f32[4,64,128]{2,1,0:T(8,128)S(1)}, f32[4,64,128]{2,1,0:T(8,128)S(1)}, f32[4,64,128]{2,1,0:T(8,128)S(1)}) custom-call(s32[1]{0:T(128)} %bitcast.refs_0_.place, f32[64,32,128]{2,1,0:T(8,128)S(1)} %copy-done.1, ...), custom_call_target="tpu_custom_call", output_to_operand_aliasing={{0}: (7, {}), {1}: (8, {}), {2}: (9, {}), {3}: (10, {})} | custom-call | tf_op jit(solution)/shard_map/outer/pallas_call | solution.py:153
  22.4 0.7 %collective-permute-start.2 = (f32[4,64,128]{2,1,0:T(8,128)S(1)}, f32[4,64,128]{2,1,0:T(8,128)S(1)}, u32[]{:S(2)}, u32[]{:S(2)}) collective-permute-start(f32[4,64,128]{2,1,0:T(8,128)S(1)} %get-tuple-element.34), channel_id=1, source_target_pairs={{0,8},{8,16},{16,24},{24,0},{1,9},{9,17},{17,25},{25,1},{2,10},{10... | collective-permute-start | bytes 393224 | tf_op jit(solution)/shard_map/ppermute | solution.py:362
  23.2 0.3 collective-permute-start.3
  23.5 0.0 collective-permute-done.8.refs_1_
  23.5 2.8 %collective-permute-start.4 = (f32[4,64,128]{2,1,0:T(8,128)S(1)}, f32[4,64,128]{2,1,0:T(8,128)S(1)}, u32[]{:S(2)}, u32[]{:S(2)}) collective-permute-start(f32[4,64,128]{2,1,0:T(8,128)S(1)} %get-tuple-element.36), channel_id=1, source_target_pairs={{0,24},{8,0},{16,8},{24,16},{1,25},{9,1},{17,9},{25,17},{2,26},{10... | collective-permute-start | bytes 393224 | tf_op jit(solution)/shard_map/ppermute | solution.py:362
  26.3 0.0 all-to-all-done.tallies_ref
  26.3 0.0 collective-permute-done.9.refs_2_
  26.3 0.0 collective-permute-done.10.refs_3_
  26.3 3.3 %analyse0.1 = (f32[256,128]{1,0:T(8,128)S(1)}, f32[256,128]{1,0:T(8,128)S(1)}, f32[256,128]{1,0:T(8,128)S(1)}, f32[256,128]{1,0:T(8,128)S(1)}) custom-call(s32[1]{0:T(128)} %bitcast.refs_0_.place, f32[8,2,8,128]{3,2,1,0:T(8,128)S(1)} %all-to-all-done.tallies_ref, f32[4,64,128]{2,1,0:T(8,128)S(1)} %get-tuple-element.41.refs_0_, ...), custom_call_target="tpu_custom_call" | custom-call | tf_op jit(solution)/shard_map/analyse0/pallas_call | solution.py:310
  29.7 1.3 %collective-permute-start.11 = (f32[256,128]{1,0:T(8,128)S(1)}, f32[256,128]{1,0:T(8,128)S(1)}, u32[]{:S(2)}, u32[]{:S(2)}) collective-permute-start(f32[256,128]{1,0:T(8,128)S(1)} %get-tuple-element.46), channel_id=1, source_target_pairs={{0,24},{8,0},{16,8},{24,16},{1,25},{9,1},{17,9},{25,17},{2,26},{10... | collective-permute-start | bytes 393224 | tf_op jit(solution)/shard_map/ppermute | solution.py:362
  30.9 0.9 %collective-permute-start.12 = (f32[256,128]{1,0:T(8,128)S(1)}, f32[256,128]{1,0:T(8,128)S(1)}, u32[]{:S(2)}, u32[]{:S(2)}) collective-permute-start(f32[256,128]{1,0:T(8,128)S(1)} %get-tuple-element.47), channel_id=1, source_target_pairs={{0,16},{8,24},{16,0},{24,8},{1,17},{9,25},{17,1},{25,9},{2,18},{10... | collective-permute-start | bytes 393224 | tf_op jit(solution)/shard_map/ppermute | solution.py:362
  31.8 0.0 collective-permute-done.2.refs_1_
  31.8 1.9 %collective-permute-start.13 = (f32[256,128]{1,0:T(8,128)S(1)}, f32[256,128]{1,0:T(8,128)S(1)}, u32[]{:S(2)}, u32[]{:S(2)}) collective-permute-start(f32[256,128]{1,0:T(8,128)S(1)} %get-tuple-element.48), channel_id=1, source_target_pairs={{0,8},{8,16},{16,24},{24,0},{1,9},{9,17},{17,25},{25,1},{2,10},{10... | collective-permute-start | bytes 393224 | tf_op jit(solution)/shard_map/ppermute | solution.py:362
  33.8 2.1 %collective-permute-done.3.refs_2_ = f32[4,64,128]{2,1,0:T(8,128)S(1)} collective-permute-done((f32[4,64,128]{2,1,0:T(8,128)S(1)}, f32[4,64,128]{2,1,0:T(8,128)S(1)}, u32[]{:S(2)}, u32[]{:S(2)}) %collective-permute-start.3) | collective-permute-done | bytes 131104 | tf_op jit(solution)/shard_map/ppermute | solution.py:362
  35.9 0.0 collective-permute-done.4.refs_3_
  35.9 3.3 %analyse1.1 = (f32[256,128]{1,0:T(8,128)S(1)}, f32[256,128]{1,0:T(8,128)S(1)}, f32[256,128]{1,0:T(8,128)S(1)}, f32[256,128]{1,0:T(8,128)S(1)}) custom-call(s32[1]{0:T(128)} %bitcast.refs_0_.place, f32[8,2,8,128]{3,2,1,0:T(8,128)S(1)} %all-to-all-done.tallies_ref, f32[4,64,128]{2,1,0:T(8,128)S(1)} %get-tuple-element.33.refs_0_, ...), custom_call_target="tpu_custom_call" | custom-call | tf_op jit(solution)/shard_map/analyse1/pallas_call | solution.py:310
  39.2 8.7 %collective-permute-start.5 = (f32[256,128]{1,0:T(8,128)S(1)}, f32[256,128]{1,0:T(8,128)S(1)}, u32[]{:S(2)}, u32[]{:S(2)}) collective-permute-start(f32[256,128]{1,0:T(8,128)S(1)} %get-tuple-element.38), channel_id=1, source_target_pairs={{0,24},{8,0},{16,8},{24,16},{1,25},{9,1},{17,9},{25,17},{2,26},{10... | collective-permute-start | bytes 393224 | tf_op jit(solution)/shard_map/ppermute | solution.py:362
  47.9 0.0 collective-permute-start.6
  47.9 0.0 collective-permute-done.11
  47.9 0.6 %collective-permute-start.7 = (f32[256,128]{1,0:T(8,128)S(1)}, f32[256,128]{1,0:T(8,128)S(1)}, u32[]{:S(2)}, u32[]{:S(2)}) collective-permute-start(f32[256,128]{1,0:T(8,128)S(1)} %get-tuple-element.40), channel_id=1, source_target_pairs={{0,8},{8,16},{16,24},{24,0},{1,9},{9,17},{17,25},{25,1},{2,10},{10... | collective-permute-start | bytes 393224 | tf_op jit(solution)/shard_map/ppermute | solution.py:362
  48.6 2.4 %collective-permute-done.12 = f32[256,128]{1,0:T(8,128)S(1)} collective-permute-done((f32[256,128]{1,0:T(8,128)S(1)}, f32[256,128]{1,0:T(8,128)S(1)}, u32[]{:S(2)}, u32[]{:S(2)}) %collective-permute-start.12) | collective-permute-done | bytes 131104 | tf_op jit(solution)/shard_map/ppermute | solution.py:362
  51.0 0.0 collective-permute-done.13
  51.0 0.8 %settle0.1.refs_4_ = f32[64,8,4,128]{3,2,1,0:T(4,128)} custom-call(s32[1]{0:T(128)} %bitcast.refs_0_.place, f32[64,4,128]{2,1,0:T(4,128)S(1)} %bitcast.13, f32[64,4,128]{2,1,0:T(4,128)S(1)} %bitcast.14, f32[64,4,128]{2,1,0:T(4,128)S(1)} %bitcast.15, f32[64,4,128]{2,1,0:T(4,128)S(1)} %bitcast.17), custom_call_target="tpu_custom_call" | custom-call | tf_op jit(solution)/shard_map/settle0/pallas_call | solution.py:338
  51.9 0.0 collective-permute-done.5
  51.9 8.7 %collective-permute-done.6 = f32[256,128]{1,0:T(8,128)S(1)} collective-permute-done((f32[256,128]{1,0:T(8,128)S(1)}, f32[256,128]{1,0:T(8,128)S(1)}, u32[]{:S(2)}, u32[]{:S(2)}) %collective-permute-start.6) | collective-permute-done | bytes 131104 | tf_op jit(solution)/shard_map/ppermute | solution.py:362
  60.6 0.0 collective-permute-done.7
  60.6 0.8 %settle1.1 = f32[64,8,4,128]{3,2,1,0:T(4,128)} custom-call(s32[1]{0:T(128)} %bitcast.refs_0_.place, f32[64,4,128]{2,1,0:T(4,128)S(1)} %bitcast.16, f32[64,4,128]{2,1,0:T(4,128)S(1)} %bitcast.18, f32[64,4,128]{2,1,0:T(4,128)S(1)} %bitcast.19, f32[64,4,128]{2,1,0:T(4,128)S(1)} %bitcast.20, ...), custom_call_target="tpu_custom_call", output_to_operand_aliasing={{}: (5, {})} | custom-call | tf_op jit(solution)/shard_map/settle1/pallas_call | solution.py:338
  (3 shorter events, 0.0 us)
Async XLA Ops:
  0.0 1.2 %copy-start = (f32[64,32,128]{2,1,0:T(8,128)S(1)}, f32[64,32,128]{2,1,0:T(8,128)}, u32[]{:S(2)}) copy-start(f32[64,32,128]{2,1,0:T(8,128)} %refs_2_.3) | copy-start | bytes 3145732
  1.2 0.8 %copy-start.2 = (f32[2,32,128]{2,1,0:T(8,128)S(1)}, f32[2,32,128]{2,1,0:T(8,128)}, u32[]{:S(2)}) copy-start(f32[2,32,128]{2,1,0:T(8,128)} %refs_4_.1) | copy-start | bytes 98308
  2.0 0.7 %copy-start.4 = (f32[32,128]{1,0:T(8,128)S(1)}, f32[32,128]{1,0:T(8,128)}, u32[]{:S(2)}) copy-start(f32[32,128]{1,0:T(8,128)} %refs_3_.3) | copy-start | bytes 49156
  2.7 18.6 %copy-start.1 = (f32[64,32,128]{2,1,0:T(8,128)S(1)}, f32[64,32,128]{2,1,0:T(8,128)}, u32[]{:S(2)}) copy-start(f32[64,32,128]{2,1,0:T(8,128)} %refs_2_.3) | copy-start | bytes 3145732
  5.2 9.7 %copy-start.7 = (f32[1280]{0:T(1024)S(1)}, f32[1280]{0:T(1024)}, u32[]{:S(2)}) copy-start(f32[1280]{0:T(1024)} %param.10) | copy-start | bytes 15364
  5.3 16.0 %collective-permute-start = (f32[4,72,128]{2,1,0:T(8,128)S(1)}, f32[4,72,128]{2,1,0:T(8,128)S(1)}, u32[]{:S(2)}, u32[]{:S(2)}) collective-permute-start(f32[4,72,128]{2,1,0:T(8,128)S(1)} %get-tuple-element.27), channel_id=1, source_target_pairs={{0,1},{1,2},{2,3},{3,4},{4,5},{5,6},{6,7},{7,0},{8,9},{9,10},{10,1... | collective-permute-start | bytes 442376 | tf_op jit(solution)/shard_map/ppermute | solution.py:367
  5.8 15.5 %collective-permute-start.1 = (f32[4,72,128]{2,1,0:T(8,128)S(1)}, f32[4,72,128]{2,1,0:T(8,128)S(1)}, u32[]{:S(2)}, u32[]{:S(2)}) collective-permute-start(f32[4,72,128]{2,1,0:T(8,128)S(1)} %get-tuple-element.28), channel_id=1, source_target_pairs={{1,0},{2,1},{3,2},{4,3},{5,4},{6,5},{7,6},{0,7},{9,8},{10,9},{11,1... | collective-permute-start | bytes 442376 | tf_op jit(solution)/shard_map/ppermute | solution.py:368
  8.7 6.2 %copy-start.8 = (f32[1280]{0:T(1024)S(1)}, f32[1280]{0:T(1024)}, u32[]{:S(2)}) copy-start(f32[1280]{0:T(1024)} %param.11) | copy-start | bytes 15364
  8.7 14.8 %collective-permute-start.8 = (f32[4,64,128]{2,1,0:T(8,128)S(1)}, f32[4,64,128]{2,1,0:T(8,128)S(1)}, u32[]{:S(2)}, u32[]{:S(2)}) collective-permute-start(f32[4,64,128]{2,1,0:T(8,128)S(1)} %get-tuple-element.42), channel_id=1, source_target_pairs={{0,8},{8,16},{16,24},{24,0},{1,9},{9,17},{17,25},{25,1},{2,10},{10... | collective-permute-start | bytes 393224 | tf_op jit(solution)/shard_map/ppermute | solution.py:362
  11.0 15.3 %collective-permute-start.9 = (f32[4,64,128]{2,1,0:T(8,128)S(1)}, f32[4,64,128]{2,1,0:T(8,128)S(1)}, u32[]{:S(2)}, u32[]{:S(2)}) collective-permute-start(f32[4,64,128]{2,1,0:T(8,128)S(1)} %get-tuple-element.43), channel_id=1, source_target_pairs={{0,16},{8,24},{16,0},{24,8},{1,17},{9,25},{17,1},{25,9},{2,18},{10... | collective-permute-start | bytes 393224 | tf_op jit(solution)/shard_map/ppermute | solution.py:362
  13.6 12.7 %collective-permute-start.10 = (f32[4,64,128]{2,1,0:T(8,128)S(1)}, f32[4,64,128]{2,1,0:T(8,128)S(1)}, u32[]{:S(2)}, u32[]{:S(2)}) collective-permute-start(f32[4,64,128]{2,1,0:T(8,128)S(1)} %get-tuple-element.44), channel_id=1, source_target_pairs={{0,24},{8,0},{16,8},{24,16},{1,25},{9,1},{17,9},{25,17},{2,26},{10... | collective-permute-start | bytes 393224 | tf_op jit(solution)/shard_map/ppermute | solution.py:362
  15.0 0.7 %copy-start.9 = (s32[1280]{0:T(1024)S(1)}, s32[1280]{0:T(1024)}, u32[]{:S(2)}) copy-start(s32[1280]{0:T(1024)} %param.13) | copy-start | bytes 15364
  15.7 0.7 %copy-start.6 = (s32[1280,1]{0,1:T(1,128)S(1)}, s32[1280,1]{0,1:T(1,128)}, u32[]{:S(2)}) copy-start(s32[1280,1]{0,1:T(1,128)} %param.12) | copy-start | bytes 15364
  17.8 3.5 %copy-start.3 = (f32[2,32,128]{2,1,0:T(8,128)S(1)}, f32[2,32,128]{2,1,0:T(8,128)}, u32[]{:S(2)}) copy-start(f32[2,32,128]{2,1,0:T(8,128)} %refs_4_.1) | copy-start | bytes 98308
  17.8 3.5 %copy-start.5 = (f32[32,128]{1,0:T(8,128)S(1)}, f32[32,128]{1,0:T(8,128)}, u32[]{:S(2)}) copy-start(f32[32,128]{1,0:T(8,128)} %refs_3_.3) | copy-start | bytes 49156
  17.8 8.5 %all-to-all-start = ((f32[8,2,8,128]{3,2,1,0:T(8,128)}), f32[8,2,8,128]{3,2,1,0:T(8,128)S(1)}, u32[]{:S(2)}, u32[]{:S(2)}) async-start(f32[8,2,8,128]{3,2,1,0:T(8,128)} %tally.1), calls=%async_computation | async-start | bytes 131072 | tf_op jit(solution)/shard_map/all_to_all | solution.py:371
  22.4 9.4 %collective-permute-start.2 = (f32[4,64,128]{2,1,0:T(8,128)S(1)}, f32[4,64,128]{2,1,0:T(8,128)S(1)}, u32[]{:S(2)}, u32[]{:S(2)}) collective-permute-start(f32[4,64,128]{2,1,0:T(8,128)S(1)} %get-tuple-element.34), channel_id=1, source_target_pairs={{0,8},{8,16},{16,24},{24,0},{1,9},{9,17},{17,25},{25,1},{2,10},{10... | collective-permute-start | bytes 393224 | tf_op jit(solution)/shard_map/ppermute | solution.py:362
  23.2 12.7 %collective-permute-start.3 = (f32[4,64,128]{2,1,0:T(8,128)S(1)}, f32[4,64,128]{2,1,0:T(8,128)S(1)}, u32[]{:S(2)}, u32[]{:S(2)}) collective-permute-start(f32[4,64,128]{2,1,0:T(8,128)S(1)} %get-tuple-element.35), channel_id=1, source_target_pairs={{0,16},{8,24},{16,0},{24,8},{1,17},{9,25},{17,1},{25,9},{2,18},{10... | collective-permute-start | bytes 393224 | tf_op jit(solution)/shard_map/ppermute | solution.py:362
  23.5 12.4 %collective-permute-start.4 = (f32[4,64,128]{2,1,0:T(8,128)S(1)}, f32[4,64,128]{2,1,0:T(8,128)S(1)}, u32[]{:S(2)}, u32[]{:S(2)}) collective-permute-start(f32[4,64,128]{2,1,0:T(8,128)S(1)} %get-tuple-element.36), channel_id=1, source_target_pairs={{0,24},{8,0},{16,8},{24,16},{1,25},{9,1},{17,9},{25,17},{2,26},{10... | collective-permute-start | bytes 393224 | tf_op jit(solution)/shard_map/ppermute | solution.py:362
  29.7 18.3 %collective-permute-start.11 = (f32[256,128]{1,0:T(8,128)S(1)}, f32[256,128]{1,0:T(8,128)S(1)}, u32[]{:S(2)}, u32[]{:S(2)}) collective-permute-start(f32[256,128]{1,0:T(8,128)S(1)} %get-tuple-element.46), channel_id=1, source_target_pairs={{0,24},{8,0},{16,8},{24,16},{1,25},{9,1},{17,9},{25,17},{2,26},{10... | collective-permute-start | bytes 393224 | tf_op jit(solution)/shard_map/ppermute | solution.py:362
  30.9 20.1 %collective-permute-start.12 = (f32[256,128]{1,0:T(8,128)S(1)}, f32[256,128]{1,0:T(8,128)S(1)}, u32[]{:S(2)}, u32[]{:S(2)}) collective-permute-start(f32[256,128]{1,0:T(8,128)S(1)} %get-tuple-element.47), channel_id=1, source_target_pairs={{0,16},{8,24},{16,0},{24,8},{1,17},{9,25},{17,1},{25,9},{2,18},{10... | collective-permute-start | bytes 393224 | tf_op jit(solution)/shard_map/ppermute | solution.py:362
  31.8 19.2 %collective-permute-start.13 = (f32[256,128]{1,0:T(8,128)S(1)}, f32[256,128]{1,0:T(8,128)S(1)}, u32[]{:S(2)}, u32[]{:S(2)}) collective-permute-start(f32[256,128]{1,0:T(8,128)S(1)} %get-tuple-element.48), channel_id=1, source_target_pairs={{0,8},{8,16},{16,24},{24,0},{1,9},{9,17},{17,25},{25,1},{2,10},{10... | collective-permute-start | bytes 393224 | tf_op jit(solution)/shard_map/ppermute | solution.py:362
  39.2 12.7 %collective-permute-start.5 = (f32[256,128]{1,0:T(8,128)S(1)}, f32[256,128]{1,0:T(8,128)S(1)}, u32[]{:S(2)}, u32[]{:S(2)}) collective-permute-start(f32[256,128]{1,0:T(8,128)S(1)} %get-tuple-element.38), channel_id=1, source_target_pairs={{0,24},{8,0},{16,8},{24,16},{1,25},{9,1},{17,9},{25,17},{2,26},{10... | collective-permute-start | bytes 393224 | tf_op jit(solution)/shard_map/ppermute | solution.py:362
  47.9 12.7 %collective-permute-start.6 = (f32[256,128]{1,0:T(8,128)S(1)}, f32[256,128]{1,0:T(8,128)S(1)}, u32[]{:S(2)}, u32[]{:S(2)}) collective-permute-start(f32[256,128]{1,0:T(8,128)S(1)} %get-tuple-element.39), channel_id=1, source_target_pairs={{0,16},{8,24},{16,0},{24,8},{1,17},{9,25},{17,1},{25,9},{2,18},{10... | collective-permute-start | bytes 393224 | tf_op jit(solution)/shard_map/ppermute | solution.py:362
  47.9 12.7 %collective-permute-start.7 = (f32[256,128]{1,0:T(8,128)S(1)}, f32[256,128]{1,0:T(8,128)S(1)}, u32[]{:S(2)}, u32[]{:S(2)}) collective-permute-start(f32[256,128]{1,0:T(8,128)S(1)} %get-tuple-element.40), channel_id=1, source_target_pairs={{0,8},{8,16},{16,24},{24,0},{1,9},{9,17},{17,25},{25,1},{2,10},{10... | collective-permute-start | bytes 393224 | tf_op jit(solution)/shard_map/ppermute | solution.py:362
